TPU v7x, 256 devices: a whole 4x4x8 slice. The times are simulated.
256 devices in a mesh: leaf: 64 (over z, x, core), front: 4 (over y).
Axes of the slice: x: 4, y: 4, z: 8, core: 2. Of those that a mesh axis runs over, the one named last changes fastest.
Arguments:
- leaf_update: float32 [32768, 512], P('leaf', 'front'), as said below
- front_entries1: float32 [4096, 1024], P('leaf', 'front'), as said below
- front_entries2: float32 [2048, 1024], replicated, as said below
- front_entries3: float32 [1024, 1024], replicated, as said below
- map_leaf: int32 [64, 4], replicated, may hold values from 0 to 7, all different within a row
- map_mid: int32 [4, 4], replicated, may hold values from 0 to 7, all different within a row
- map_top: int32 [2, 4], replicated, may hold values from 0 to 7, as said below
Outputs:
- leaf_inverse: float32 [32768, 512], P('leaf', 'front')
Inputs may be any that keep to these rules, and one draw needn't show every extreme that they name: `map_leaf`: row s gives, for each block of 128 rows of subtree s's update, the block of its first level front that receives it; the entries of a row are distinct. `map_mid`: row k gives, for each block of 128 rows of the update of first level node k, the block of second level front k // 2 that receives it; the entries of a row are distinct. `map_top`: row n gives, for each block of 128 rows of the update of second level node n, the block of the top front that receives it; the entries of a row are distinct, and every block of the top front is named by at least one of the two rows. `leaf_update`: each block of 512 rows is symmetric and positive definite. `front_entries1`: each front's block is symmetric and positive definite. `front_entries2`: each front's block is symmetric and positive definite. `front_entries3`: symmetric and positive definite.
All inputs are finite; a program needn't handle non-finite values.
Results may differ from a plain program's by a relative error of at most 0.00017.
Values sent between devices are 32-bit elements; how exact they have to be, the bound alone decides.
A program may use at most 128 MiB of HBM per device.

v0:
```python
import jax
import jax.numpy as jnp
from jax import lax
from jax.sharding import PartitionSpec as P

BLK = 128
SEP1 = 512
SEP2 = 512
SEP3 = 1024
RUP = 512


def partner_2(block, axis, distance):
    count = lax.axis_size(axis)
    route = []
    for low in range(count):
        high = low | 1 << distance
        if high != low and high < count:
            route += [(low, high), (high, low)]
    return lax.ppermute(block, axis, route)


def laid_out(tiles, dim):
    dims = list(tiles.shape[1:])
    dims[dim] *= tiles.shape[0]
    return jnp.moveaxis(tiles, 0, dim).reshape(dims)


def sent_to_all(shard, axis):
    copies = jnp.broadcast_to(shard, (lax.axis_size(axis), *shard.shape))
    return lax.all_to_all(copies, axis, split_axis=0, concat_axis=0, tiled=True)


def gathered_copies(shard, axis, dim):
    return laid_out(sent_to_all(shard, axis), dim)


def side_by_side(arrays, axis, dim, along):
    ends, at = ([], 0)
    for a in arrays[:-1]:
        at += a.shape[along]
        ends.append(at)
    both = jnp.concatenate(arrays, axis=along)
    return tuple(jnp.split(gathered_copies(both, axis, dim), ends, axis=along))


def product(left_side, right_side):
    return jnp.dot(left_side, right_side, precision=lax.Precision.HIGHEST)


def selector(block_list, parent_blocks):
    return (block_list[:, None] == jnp.arange(parent_blocks, dtype=jnp.int32)[None, :]).astype(
        jnp.float32
    )


def placement(block_list, parent_blocks):
    child_blocks = block_list.shape[0]
    hits = (block_list[:, None] == jnp.arange(parent_blocks, dtype=jnp.int32)[None, :]).astype(
        jnp.int32
    )
    source = jnp.sum(hits * jnp.arange(child_blocks, dtype=jnp.int32)[:, None], axis=0)
    present = jnp.sum(hits, axis=0).astype(jnp.float32)
    return (source, present)


def extend(update, block_list, parent_blocks):
    child_blocks = block_list.shape[0]
    block_rows = update.shape[0] // child_blocks
    source, present = placement(block_list, parent_blocks)
    blocked = update.reshape(child_blocks, block_rows, child_blocks, block_rows)
    picked_rows = jnp.take(blocked, source, axis=0)
    picked = jnp.take(picked_rows, source, axis=2)
    weight = present[:, None, None, None] * present[None, None, :, None]
    result = picked * weight
    return result.reshape(parent_blocks * block_rows, parent_blocks * block_rows)


def extract(sigma, block_list, parent_blocks):
    child_blocks = block_list.shape[0]
    block_rows = sigma.shape[0] // parent_blocks
    blocked = sigma.reshape(parent_blocks, block_rows, parent_blocks, block_rows)
    picked_rows = jnp.take(blocked, block_list, axis=0)
    picked = jnp.take(picked_rows, block_list, axis=2)
    return picked.reshape(child_blocks * block_rows, child_blocks * block_rows)


def expand(picker, block_rows):
    child_blocks, parent_blocks = picker.shape
    identity = jnp.eye(block_rows, dtype=jnp.float32)
    result = jnp.einsum("ia,xy->axiy", picker, identity, precision=lax.Precision.HIGHEST)
    return result.reshape(parent_blocks * block_rows, child_blocks * block_rows)


def factor(assembled, separator):
    factor_ss = jnp.linalg.cholesky(assembled[:separator, :separator])
    solved = lax.linalg.triangular_solve(
        factor_ss, assembled[:separator, separator:], left_side=True, lower=True
    )
    factor_rs = solved.T
    update = assembled[separator:, separator:] - product(factor_rs, solved)
    return (factor_ss, factor_rs, update)


def inverse(factor_ss, factor_rs, sigma_rr):
    separator = factor_ss.shape[0]
    identity = jnp.eye(separator, dtype=jnp.float32)
    inverse_ss = lax.linalg.triangular_solve(factor_ss, identity, left_side=True, lower=True)
    coupling = product(factor_rs, inverse_ss)
    sigma_rs = -product(sigma_rr, coupling)
    sigma_ss = product(inverse_ss.T, inverse_ss) - product(coupling.T, sigma_rs)
    upper_rows = jnp.concatenate([sigma_ss, sigma_rs.T], axis=1)
    lower_rows = jnp.concatenate([sigma_rs, sigma_rr], axis=1)
    return jnp.concatenate([upper_rows, lower_rows], axis=0)


def ascend(update_share, bit_number, entries, block_maps, child_index, parent_blocks):
    partner = partner_2(update_share, "leaf", bit_number)
    mine_full, partner_full = side_by_side((update_share, partner), "front", 1, 0)
    lower_side = child_index % 2 == 0
    left_update = jnp.where(lower_side, mine_full, partner_full)
    right_update = jnp.where(lower_side, partner_full, mine_full)
    first_child = child_index - child_index % 2
    assembled = entries + extend(left_update, block_maps[first_child], parent_blocks)
    return assembled + extend(right_update, block_maps[first_child + 1], parent_blocks)


def body(leaf_update, front_entries1, front_entries2, front_entries3, map_leaf, map_mid, map_top):
    leaf_index = lax.axis_index("leaf")
    column = lax.axis_index("front")
    members = lax.axis_size("leaf") // 4
    low_bits = members.bit_length() - 1
    first_node = leaf_index // members
    second_node = leaf_index // (2 * members)
    order_one = SEP1 + RUP
    order_two = SEP2 + RUP
    update = gathered_copies(leaf_update, "front", 1)
    leaf_blocks = map_leaf[leaf_index]
    spread = extend(update, leaf_blocks, order_one // BLK)
    share_width = front_entries1.shape[1]
    column_share = lax.dynamic_slice_in_dim(spread, column * share_width, share_width, 1)
    entry_rows = front_entries1.shape[0]
    offset = leaf_index % members * entry_rows
    with_entries = lax.dynamic_slice_in_dim(column_share, offset, entry_rows, 0) + front_entries1
    column_share = lax.dynamic_update_slice_in_dim(column_share, with_entries, offset, 0)
    for bit_number in range(low_bits):
        halfway = column_share.shape[0] // 2
        upper_side = leaf_index >> bit_number & 1 == 1
        kept_rows = jnp.where(upper_side, column_share[halfway:], column_share[:halfway])
        sent_rows = jnp.where(upper_side, column_share[:halfway], column_share[halfway:])
        column_share = kept_rows + partner_2(sent_rows, "leaf", bit_number)
    for bit_number in reversed(range(low_bits)):
        upper_side = leaf_index >> bit_number & 1 == 1
        partner_rows = partner_2(column_share, "leaf", bit_number)
        column_share = jnp.where(
            upper_side,
            jnp.concatenate([partner_rows, column_share], axis=0),
            jnp.concatenate([column_share, partner_rows], axis=0),
        )
    front_one = lax.all_gather(column_share, "front", axis=1, tiled=True)
    factor_one, coupling_one, update_one = factor(front_one, SEP1)
    update_width = update_one.shape[1] // lax.axis_size("front")
    update_share = lax.dynamic_slice_in_dim(update_one, column * update_width, update_width, 1)
    entries_two = lax.dynamic_slice_in_dim(front_entries2, second_node * order_two, order_two, 0)
    front_two = ascend(update_share, low_bits, entries_two, map_mid, first_node, order_two // BLK)
    factor_two, coupling_two, update_two = factor(front_two, SEP2)
    update_share = lax.dynamic_slice_in_dim(update_two, column * update_width, update_width, 1)
    front_three = ascend(
        update_share, low_bits + 1, front_entries3, map_top, second_node, SEP3 // BLK
    )
    factor_top = jnp.linalg.cholesky(front_three)
    basis = expand(selector(map_top[second_node], SEP3 // BLK), BLK)
    solved = lax.linalg.triangular_solve(factor_top, basis, left_side=True, lower=True)
    sigma_rr = product(solved.T, solved)
    sigma_two = inverse(factor_two, coupling_two, sigma_rr)
    sigma_rr = extract(sigma_two, map_mid[first_node], order_two // BLK)
    sigma_one = inverse(factor_one, coupling_one, sigma_rr)
    selected = extract(sigma_one, leaf_blocks, order_one // BLK)
    out_width = leaf_update.shape[1]
    return lax.dynamic_slice_in_dim(selected, column * out_width, out_width, 1)


def solution(mesh):
    in_specs = (P("leaf", "front"), P("leaf", "front"), P(), P(), P(), P(), P())
    out_specs = P("leaf", "front")
    return jax.shard_map(body, mesh=mesh, in_specs=in_specs, out_specs=out_specs, check_vma=False)
```

profile of v0, /device:TPU:1, one launch (start us, length us, event | category | flops | bytes accessed | tf_op | source)
XLA Modules:
  0.0 1032.5 jit_solution(12742056882769920777)
XLA Ops:
  14.9 12.2 %all-to-all-done = f32[4,512,128]{2,1,0:T(8,128)S(1)} async-done(((f32[4,512,128]{2,1,0:T(8,128)}), f32[4,512,128]{2,1,0:T(8,128)S(1)}, u32[]{:S(2)}, u32[]{:S(2)}) %all-to-all-start) | async-done | bytes 1048608 | tf_op jit(solution)/shard_map/all_to_all | solution.py:31
  107.2 40.6 %all-gather.2.cloned.1.call-done = f32[1024,1024]{0,1:T(8,128)} async-done(((f32[1024,256]{0,1:T(8,128)}), f32[1024,1024]{0,1:T(8,128)}) %all-gather.2.cloned.1.call-update) | async-done | bytes 4194320 | tf_op jit(solution)/shard_map/all_gather | solution.py:160
  152.5 11.7 %cholesky.761 = f32[128,128]{1,0:T(8,128)S(1)} custom-call(f32[128,128]{1,0:T(8,128)S(1)} %cholesky.871), custom_call_target="Cholesky" | custom-call | tf_op jit(solution)/shard_map/jit(cholesky)/cholesky | solution.py:96
  164.3 9.8 custom-call.87
  174.8 11.9 %cholesky.773 = f32[128,128]{1,0:T(8,128)S(1)} custom-call(f32[128,128]{1,0:T(8,128)S(1)} %cholesky.875), custom_call_target="Cholesky" | custom-call | tf_op jit(solution)/shard_map/jit(cholesky)/cholesky | solution.py:96
  186.8 9.8 custom-call.88
  197.2 11.7 %cholesky.790 = f32[128,128]{1,0:T(8,128)S(1)} custom-call(f32[128,128]{1,0:T(8,128)S(1)} %cholesky.880), custom_call_target="Cholesky" | custom-call | tf_op jit(solution)/shard_map/jit(cholesky)/cholesky | solution.py:96
  220.1 12.1 %cholesky.803 = f32[128,128]{1,0:T(8,128)S(1)} custom-call(f32[128,128]{1,0:T(8,128)S(1)} %convolution_subtract_fusion.30), custom_call_target="Cholesky" | custom-call | tf_op jit(solution)/shard_map/jit(cholesky)/cholesky | solution.py:96
  244.6 39.3 %custom-call.90 = f32[4,128,128]{1,2,0:T(8,128)S(1)} custom-call(f32[4,128,128]{2,1,0:T(8,128)S(1)} %get-tuple-element.48), custom_call_target="InvertDiagBlocksLowerTriangular" | custom-call | tf_op jit(solution)/shard_map/triangular_solve/custom-call.19 | solution.py:108
  335.9 13.1 %all-to-all-done.1 = f32[4,1024,128]{2,1,0:T(8,128)S(1)} async-done(((f32[4,1024,128]{2,1,0:T(8,128)}), f32[4,1024,128]{2,1,0:T(8,128)S(1)}, u32[]{:S(2)}, u32[]{:S(2)}) %all-to-all-start.1) | async-done | bytes 2097184 | tf_op jit(solution)/shard_map/all_to_all | solution.py:31
  396.1 11.7 %cholesky.818 = f32[128,128]{1,0:T(8,128)S(1)} custom-call(f32[128,128]{1,0:T(8,128)S(1)} %cholesky.884), custom_call_target="Cholesky" | custom-call | tf_op jit(solution)/shard_map/jit(cholesky)/cholesky | solution.py:96
  408.5 9.8 custom-call.92
  419.7 12.1 %cholesky.830 = f32[128,128]{1,0:T(8,128)S(1)} custom-call(f32[128,128]{1,0:T(8,128)S(1)} %cholesky.888), custom_call_target="Cholesky" | custom-call | tf_op jit(solution)/shard_map/jit(cholesky)/cholesky | solution.py:96
  445.8 13.2 %cholesky.847 = f32[128,128]{1,0:T(8,128)} custom-call(f32[128,128]{1,0:T(8,128)} %cholesky.893), custom_call_target="Cholesky" | custom-call | tf_op jit(solution)/shard_map/jit(cholesky)/cholesky | solution.py:96
  461.2 11.3 %custom-call.94 = f32[1,128,128]{1,2,0:T(8,128)} custom-call(f32[1,128,128]{2,1,0:T(8,128)} %get-tuple-element.160), custom_call_target="InvertDiagBlocksLowerTriangular" | custom-call | tf_op jit(solution)/shard_map/jit(cholesky)/cholesky/custom-call.2 | solution.py:96
  473.9 11.9 %cholesky.860 = f32[128,128]{1,0:T(8,128)S(1)} custom-call(f32[128,128]{1,0:T(8,128)S(1)} %convolution_subtract_fusion.29), custom_call_target="Cholesky" | custom-call | tf_op jit(solution)/shard_map/jit(cholesky)/cholesky | solution.py:96
  497.5 39.3 %custom-call.95 = f32[4,128,128]{1,2,0:T(8,128)S(1)} custom-call(f32[4,128,128]{2,1,0:T(8,128)S(1)} %get-tuple-element.50), custom_call_target="InvertDiagBlocksLowerTriangular" | custom-call | tf_op jit(solution)/shard_map/triangular_solve/custom-call.19 | solution.py:108
  580.6 10.2 all-to-all-done.2
  645.9 11.7 %cholesky.353 = f32[128,128]{1,0:T(8,128)S(1)} custom-call(f32[128,128]{1,0:T(8,128)S(1)} %cholesky.897), custom_call_target="Cholesky" | custom-call | tf_op jit(solution)/shard_map/jit(cholesky)/cholesky | solution.py:171
  660.1 9.8 custom-call.67
  673.9 11.9 %cholesky.374 = f32[128,128]{1,0:T(8,128)S(1)} custom-call(f32[128,128]{1,0:T(8,128)S(1)} %cholesky.901), custom_call_target="Cholesky" | custom-call | tf_op jit(solution)/shard_map/jit(cholesky)/cholesky | solution.py:171
  687.8 9.8 custom-call.68
  701.0 11.7 %cholesky.401 = f32[128,128]{1,0:T(8,128)S(1)} custom-call(f32[128,128]{1,0:T(8,128)S(1)} %cholesky.906), custom_call_target="Cholesky" | custom-call | tf_op jit(solution)/shard_map/jit(cholesky)/cholesky | solution.py:171
  727.3 12.1 %cholesky.603 = f32[128,128]{1,0:T(8,128)S(1)} custom-call(f32[128,128]{1,0:T(8,128)S(1)} %cholesky.911), custom_call_target="Cholesky" | custom-call | tf_op jit(solution)/shard_map/jit(cholesky)/cholesky | solution.py:171
  754.0 11.7 %cholesky.622 = f32[128,128]{1,0:T(8,128)S(1)} custom-call(f32[128,128]{1,0:T(8,128)S(1)} %cholesky.916), custom_call_target="Cholesky" | custom-call | tf_op jit(solution)/shard_map/jit(cholesky)/cholesky | solution.py:171
  767.1 9.9 custom-call.97
  780.4 11.7 %cholesky.638 = f32[128,128]{1,0:T(8,128)S(1)} custom-call(f32[128,128]{1,0:T(8,128)S(1)} %cholesky.921), custom_call_target="Cholesky" | custom-call | tf_op jit(solution)/shard_map/jit(cholesky)/cholesky | solution.py:171
  793.4 9.8 custom-call.98
  806.2 11.9 %cholesky.654 = f32[128,128]{1,0:T(8,128)S(1)} custom-call(f32[128,128]{1,0:T(8,128)S(1)} %cholesky.926), custom_call_target="Cholesky" | custom-call | tf_op jit(solution)/shard_map/jit(cholesky)/cholesky | solution.py:171
  831.9 11.7 %cholesky.668 = f32[128,128]{1,0:T(8,128)S(1)} custom-call(f32[128,128]{1,0:T(8,128)S(1)} %convolution_subtract_fusion.28), custom_call_target="Cholesky" | custom-call | tf_op jit(solution)/shard_map/jit(cholesky)/cholesky | solution.py:171
  854.7 28.9 %while.9 = (s32[]{:T(128)}, f32[1024,1024]{1,0:T(8,128)}, s32[8,2]{0,1:T(2,128)S(1)}, f32[8,128,128]{2,1,0:T(8,128)}, s32[]{:T(128)}) while((s32[]{:T(128)}, f32[1024,1024]{1,0:T(8,128)}, s32[8,2]{0,1:T(2,128)S(1)}, f32[8,128,128]{2,1,0:T(8,128)}, s32[]{:T(128)}) %tuple.145), condition=%wide.while_cond.1, body=%wide.while_body.1.sunk | while | flops 2 | bytes 132705 | solution.py:173
  883.6 79.8 %custom-call.71 = f32[8,128,128]{1,2,0:T(8,128)S(1)} custom-call(f32[8,128,128]{2,1,0:T(8,128)} %get-tuple-element.29), custom_call_target="InvertDiagBlocksLowerTriangular" | custom-call | tf_op jit(solution)/shard_map/triangular_solve | solution.py:173
  (478 shorter events, 518.1 us)
Async XLA Ops:
  8.6 18.5 %all-to-all-start = ((f32[4,512,128]{2,1,0:T(8,128)}), f32[4,512,128]{2,1,0:T(8,128)S(1)}, u32[]{:S(2)}, u32[]{:S(2)}) async-start(f32[4,512,128]{2,1,0:T(8,128)} %broadcast_in_dim.39), calls=%async_computation | async-start | bytes 2097152 | tf_op jit(solution)/shard_map/all_to_all | solution.py:31
  13.6 134.3 %all-gather.2.cloned.1.call-start = ((), (), s32[]{:S(2)}) async-start(), calls=%async_computation.3 | async-start | bytes 5242880 | tf_op jit(solution)/shard_map/all_gather | solution.py:160
  48.6 3.9 collective-permute-start
  52.7 43.2 %copy-start.57 = (s32[4,4]{1,0:T(4,128)S(1)}, s32[4,4]{1,0:T(4,128)}, u32[]{:S(2)}) copy-start(s32[4,4]{1,0:T(4,128)} %param.29) | copy-start | bytes 196
  52.7 43.4 %copy-start.55 = (s32[2,4]{1,0:T(2,128)S(1)}, s32[2,4]{1,0:T(2,128)}, u32[]{:S(2)}) copy-start(s32[2,4]{1,0:T(2,128)} %param.30) | copy-start | bytes 100
  52.7 7.6 collective-permute-start.1
  60.4 5.4 collective-permute-start.2
  65.9 4.1 collective-permute-start.3
  70.1 4.0 collective-permute-start.4
  74.2 5.4 collective-permute-start.5
  79.6 6.7 collective-permute-start.6
  86.4 8.1 collective-permute-start.7
  152.4 83.7 %copy-start.59 = (s32[4]{0:T(128)S(1)}, s32[4]{0:T(128)}, u32[]{:S(2)}) copy-start(s32[4]{0:T(128)} %iota_multiply_fusion) | copy-start | bytes 52
  244.5 50.0 %copy-start.4 = (f32[512,512]{1,0:T(8,128)}, f32[512,512]{1,0:T(8,128)S(1)}, u32[]{:S(2)}) copy-start(f32[512,512]{1,0:T(8,128)S(1)} %get-tuple-element.338) | copy-start | bytes 3145732
  295.6 21.9 %collective-permute-start.8 = (f32[512,128]{0,1:T(8,128)S(1)}, f32[512,128]{0,1:T(8,128)}, u32[]{:S(2)}, u32[]{:S(2)}) collective-permute-start(f32[512,128]{0,1:T(8,128)S(1)} %dynamic-slice_subtract_fusion.1), channel_id=1, source_target_pairs={{0,64},{64,0},{4,68},{68,4},{8,72},{72,8},{12,76},{76,12},{16,80},... | collective-permute-start | bytes 786440 | tf_op jit(solution)/shard_map/ppermute | solution.py:20
  320.2 28.9 %all-to-all-start.1 = ((f32[4,1024,128]{2,1,0:T(8,128)}), f32[4,1024,128]{2,1,0:T(8,128)S(1)}, u32[]{:S(2)}, u32[]{:S(2)}) async-start(f32[4,1024,128]{2,1,0:T(8,128)} %broadcast_in_dim.40), calls=%async_computation.1 | async-start | bytes 4194304 | tf_op jit(solution)/shard_map/all_to_all | solution.py:31
  497.5 50.4 %copy-start.5 = (f32[512,512]{1,0:T(8,128)}, f32[512,512]{1,0:T(8,128)S(1)}, u32[]{:S(2)}) copy-start(f32[512,512]{1,0:T(8,128)S(1)} %get-tuple-element.339) | copy-start | bytes 3145732
  536.8 18.8 %copy-start.21 = (f32[4,128,128]{1,2,0:T(8,128)}, f32[4,128,128]{1,2,0:T(8,128)S(1)}, u32[]{:S(2)}) copy-start(f32[4,128,128]{1,2,0:T(8,128)S(1)} %custom-call.95) | copy-start | bytes 786436
  538.3 14.3 %copy-start.10 = (f32[128,512]{1,0:T(8,128)S(1)}, f32[128,512]{1,0:T(8,128)}, u32[]{:S(2)}) copy-start(f32[128,512]{1,0:T(8,128)} %fusion.95) | copy-start | bytes 786436
  538.3 14.3 %copy-start.15 = (f32[128,512]{1,0:T(8,128)S(1)}, f32[128,512]{1,0:T(8,128)}, u32[]{:S(2)}) copy-start(f32[128,512]{1,0:T(8,128)} %copy-done.14) | copy-start | bytes 786436
  538.3 14.3 %copy-start.17 = (f32[128,512]{1,0:T(8,128)S(1)}, f32[128,512]{1,0:T(8,128)}, u32[]{:S(2)}) copy-start(f32[128,512]{1,0:T(8,128)} %copy-done.16) | copy-start | bytes 786436
  538.3 14.3 %copy-start.25 = (f32[128,512]{1,0:T(8,128)S(1)}, f32[128,512]{1,0:T(8,128)}, u32[]{:S(2)}) copy-start(f32[128,512]{1,0:T(8,128)} %copy-done.24) | copy-start | bytes 786436
  538.3 14.3 %copy-start.37 = (f32[128,512]{1,0:T(8,128)S(1)}, f32[128,512]{1,0:T(8,128)}, u32[]{:S(2)}) copy-start(f32[128,512]{1,0:T(8,128)} %copy-done.36) | copy-start | bytes 786436
  538.3 14.3 %copy-start.47 = (f32[128,512]{1,0:T(8,128)S(1)}, f32[128,512]{1,0:T(8,128)}, u32[]{:S(2)}) copy-start(f32[128,512]{1,0:T(8,128)} %copy-done.46) | copy-start | bytes 786436
  540.5 15.1 %copy-start.18 = (f32[128,512]{1,0:T(8,128)}, f32[128,512]{1,0:T(8,128)S(1)}, u32[]{:S(2)}) copy-start(f32[128,512]{1,0:T(8,128)S(1)} %fusion.174) | copy-start | bytes 786436
  545.9 15.1 %copy-start.50 = (f32[128,512]{1,0:T(8,128)}, f32[128,512]{1,0:T(8,128)S(1)}, u32[]{:S(2)}) copy-start(f32[128,512]{1,0:T(8,128)S(1)} %fusion.178) | copy-start | bytes 786436
  548.8 12.2 %collective-permute-start.9 = (f32[512,128]{0,1:T(8,128)S(1)}, f32[512,128]{0,1:T(8,128)S(1)}, u32[]{:S(2)}, u32[]{:S(2)}) collective-permute-start(f32[512,128]{0,1:T(8,128)S(1)} %dynamic-slice_subtract_fusion), channel_id=1, source_target_pairs={{0,128},{128,0},{4,132},{132,4},{8,136},{136,8},{12,140},{140,12},... | collective-permute-start | bytes 786440 | tf_op jit(solution)/shard_map/ppermute | solution.py:20
  562.8 28.1 %all-to-all-start.2 = ((f32[4,1024,128]{2,1,0:T(8,128)}), f32[4,1024,128]{2,1,0:T(8,128)S(1)}, u32[]{:S(2)}, u32[]{:S(2)}) async-start(f32[4,1024,128]{2,1,0:T(8,128)} %broadcast_in_dim.41), calls=%async_computation.2 | async-start | bytes 4194304 | tf_op jit(solution)/shard_map/all_to_all | solution.py:31
  849.8 113.6 %copy-start.20 = (f32[1,128,4,128]{1,3,2,0:T(8,128)S(1)}, f32[1,128,4,128]{1,3,2,0:T(8,128)}, u32[]{:S(2)}) copy-start(f32[1,128,4,128]{1,3,2,0:T(8,128)} %get-tuple-element.105) | copy-start | bytes 786436
  849.8 114.1 %copy-start.33 = (f32[128,512]{1,0:T(8,128)S(1)}, f32[128,512]{1,0:T(8,128)}, u32[]{:S(2)}) copy-start(f32[128,512]{1,0:T(8,128)} %copy.201) | copy-start | bytes 786436
  854.7 111.0 %copy-start.35 = (f32[128,512]{1,0:T(8,128)S(1)}, f32[128,512]{1,0:T(8,128)}, u32[]{:S(2)}) copy-start(f32[128,512]{1,0:T(8,128)} %copy.202) | copy-start | bytes 786436
  854.7 112.8 %copy-start.34 = (f32[128,512]{1,0:T(8,128)S(1)}, f32[128,512]{1,0:T(8,128)}, u32[]{:S(2)}) copy-start(f32[128,512]{1,0:T(8,128)} %copy.203) | copy-start | bytes 786436
  (42 other events, 262.2 us)
Sparse Core Ops, SparseCore 0:
  95.9 51.8 all-gather.1
where the time goes:
time: 1050 us; the launch traced here: 1030 us
  other arithmetic  573 us (55%)
  local copies, waits for them, and re-layouts  179 us (17%)
  matrix products  110 us (10%)
  waiting for transfers between devices  106 us (10%)
  starting transfers between devices  39.5 us (4%)
  between operations  25.6 us (2%)
    another operation x31, other arithmetic, body(): factor_top = jnp.linalg.cholesky(front_three)  173 us
    another operation x29, other arithmetic, factor(): factor_ss = jnp.linalg.cholesky(assembled[:separator, :separator])  164 us
    another operation x3, other arithmetic, body(): lax.linalg.triangular_solve(factor_top, basis, left_side=True, lower=True)  85.2 us
    another operation x5, other arithmetic, inverse(): lax.linalg.triangular_solve(factor_ss, identity, left_side=True, lower=True)  79.5 us
    all_gather x1, waiting for transfers between devices, body(): front_one = lax.all_gather(column_share, 'front', axis=1, tiled=True)  40.6 us
    all_to_all x3, waiting for transfers between devices, sent_to_all(): return lax.all_to_all(copies, axis, split_axis=0, concat_axis=0, tiled=True)  35.4 us
    ppermute x10, waiting for transfers between devices, partner_2(): return lax.ppermute(block, axis, route)  29.7 us
    another operation x25, local copies, waits for them, and re-layouts  29 us
  transfers between devices with their start and end apart: 14, of which 13 were waited for; matrix products, arithmetic and copies ran while one was open for 6% of the time, Pallas kernels for 0%

commit v1 on v0

v1 whole, which is shorter than its diff:
```python
import functools

import jax
import jax.numpy as jnp
from jax import lax
from jax.experimental import pallas as pl
from jax.experimental.pallas import tpu as pltpu
from jax.sharding import PartitionSpec as P

BLK = 128
SEP1 = 512
SEP2 = 512
SEP3 = 1024
RUP = 512


def partner_2(block, axis, distance):
    count = lax.axis_size(axis)
    route = []
    for low in range(count):
        high = low | 1 << distance
        if high != low and high < count:
            route += [(low, high), (high, low)]
    return lax.ppermute(block, axis, route)


def laid_out(tiles, dim):
    dims = list(tiles.shape[1:])
    dims[dim] *= tiles.shape[0]
    return jnp.moveaxis(tiles, 0, dim).reshape(dims)


def sent_to_all(shard, axis):
    copies = jnp.broadcast_to(shard, (lax.axis_size(axis), *shard.shape))
    return lax.all_to_all(copies, axis, split_axis=0, concat_axis=0, tiled=True)


def gathered_copies(shard, axis, dim):
    return laid_out(sent_to_all(shard, axis), dim)


def side_by_side(arrays, axis, dim, along):
    ends, at = ([], 0)
    for a in arrays[:-1]:
        at += a.shape[along]
        ends.append(at)
    both = jnp.concatenate(arrays, axis=along)
    return tuple(jnp.split(gathered_copies(both, axis, dim), ends, axis=along))


def product(left_side, right_side):
    return jnp.dot(left_side, right_side, precision=lax.Precision.HIGHEST)


def placement(block_list, parent_blocks):
    child_blocks = block_list.shape[0]
    hits = (block_list[:, None] == jnp.arange(parent_blocks, dtype=jnp.int32)[None, :]).astype(
        jnp.int32
    )
    source = jnp.sum(hits * jnp.arange(child_blocks, dtype=jnp.int32)[:, None], axis=0)
    present = jnp.sum(hits, axis=0).astype(jnp.float32)
    return (source, present)


def extend(update, block_list, parent_blocks):
    child_blocks = block_list.shape[0]
    block_rows = update.shape[0] // child_blocks
    source, present = placement(block_list, parent_blocks)
    blocked = update.reshape(child_blocks, block_rows, child_blocks, block_rows)
    picked_rows = jnp.take(blocked, source, axis=0)
    picked = jnp.take(picked_rows, source, axis=2)
    weight = present[:, None, None, None] * present[None, None, :, None]
    result = picked * weight
    return result.reshape(parent_blocks * block_rows, parent_blocks * block_rows)


F32, BF16 = jnp.float32, jnp.bfloat16


def row_of(x, k):
    return jnp.broadcast_to(x[k : k + 1, :], (8, 128))


def pick_row(x, k):
    return jnp.take_along_axis(x, jnp.full((8, 128), k, jnp.int32), axis=0)


def along(x, lanes):
    return jnp.take_along_axis(x, lanes, axis=1)


def invert(w):
    lane = lax.broadcasted_iota(jnp.int32, (8, 128), 1)
    sub = lax.broadcasted_iota(jnp.int32, (8, 128), 0)
    tiles = [w[8 * i : 8 * i + 8, :] for i in range(16)]
    diagonal = [jnp.where(lane == 8 * i + sub, x, 0.0) for i, x in enumerate(tiles)]
    total = functools.reduce(jnp.add, diagonal)
    across = lax.rsqrt(jnp.broadcast_to(jnp.sum(total, axis=0, keepdims=True), (8, 128)))
    down = [
        lax.rsqrt(jnp.broadcast_to(jnp.sum(x, axis=1, keepdims=True), (8, 128))) for x in diagonal
    ]
    for i in range(16):
        w[8 * i : 8 * i + 8, :] = tiles[i] * down[i] * across

    def panel(p, carry):
        base = 8 * p
        here = pl.ds(pl.multiple_of(base, 8), 8)
        tiles = [w[8 * i : 8 * i + 8, :] for i in range(16)]
        pivot = w[here, :]
        for k in range(0, 8, 2):
            c = jnp.full((8, 128), base + k, jnp.int32)
            at_first, at_second = lane == c, lane == c + 1
            hit = at_first | at_second
            first, second = along(pivot, c), along(pivot, c + 1)
            a, b, d = pick_row(first, k), pick_row(first, k + 1), pick_row(second, k + 1)
            upper = jnp.where(at_first, -1.0, jnp.where(at_second, 0.0, row_of(pivot, k)))
            lower = jnp.where(at_second, -1.0, jnp.where(at_first, 0.0, row_of(pivot, k + 1)))
            scale = 1.0 / (a * d - b * b)
            new_first = (d * upper - b * lower) * scale
            new_second = (a * lower - b * upper) * scale
            tiles = [
                jnp.where(hit, 0.0, x) - along(x, c) * new_first - along(x, c + 1) * new_second
                for x in tiles
            ]
            pivot = jnp.where(hit, 0.0, pivot) - first * new_first - second * new_second
            pivot = jnp.where(sub == k, new_first, jnp.where(sub == k + 1, new_second, pivot))
        for i in range(16):
            w[8 * i : 8 * i + 8, :] = tiles[i]
        w[here, :] = pivot
        return carry

    lax.fori_loop(0, 16, panel, 0)
    for i in range(16):
        w[8 * i : 8 * i + 8, :] = -w[8 * i : 8 * i + 8, :] * down[i] * across


def halves(x):
    high = x.astype(BF16)
    return high, (x - high.astype(F32)).astype(BF16)


def put_left(ref, rows, x):
    high, low = halves(x)
    width = x.shape[1]
    ref[rows, :width] = high
    ref[rows, width : 2 * width] = high
    ref[rows, 2 * width : 3 * width] = low
    if ref.shape[1] > 3 * width:
        ref[rows, 3 * width :] = low


def put_right(ref, columns, x):
    high, low = halves(x)
    depth = x.shape[0]
    ref[:depth, columns] = high
    ref[depth : 2 * depth, columns] = low
    ref[2 * depth : 3 * depth, columns] = high
    if ref.shape[0] > 3 * depth:
        ref[3 * depth :, columns] = low


def dot(a, b):
    return jnp.dot(a, b, preferred_element_type=F32)


def eliminate(o, blocks, left, right, small_left, small_right, inverted, new_rows, new_columns):
    n = o.shape[0]
    whole = slice(None)

    def step(j, carry):
        at = pl.ds(pl.multiple_of(j * BLK, BLK), BLK)
        inverted[...] = o[at, at]
        invert(inverted)
        block = inverted[...]
        put_left(small_left, whole, block)
        put_right(small_right, whole, block)
        put_right(right, whole, o[at, :])
        put_left(left, whole, o[:, at])
        new_rows[...] = dot(small_left[...], right[...])

        def column_tile(t, carry):
            these = pl.ds(pl.multiple_of(t * 256, 256), 256)
            new_columns[these, :] = dot(left[these, :], small_right[...])
            return carry

        lax.fori_loop(0, n // 256, column_tile, 0)
        put_right(right, whole, new_rows[...])

        def tile(t, carry):
            these = pl.ds(pl.multiple_of(t * 256, 256), 256)
            o[these, :] = o[these, :] - dot(left[these, :], right[...])
            return carry

        lax.fori_loop(0, n // 256, tile, 0)
        o[:, at] = new_columns[...]
        o[at, :] = new_rows[...]
        o[at, at] = -inverted[...]
        return carry

    lax.fori_loop(0, blocks, step, 0)


def scratch_for(n):
    return [
        pltpu.VMEM((n, 4 * BLK), BF16),
        pltpu.VMEM((4 * BLK, n), BF16),
        pltpu.VMEM((BLK, 4 * BLK), BF16),
        pltpu.VMEM((4 * BLK, BLK), BF16),
        pltpu.VMEM((BLK, BLK), F32),
        pltpu.VMEM((BLK, n), F32),
        pltpu.VMEM((n, BLK), F32),
    ]


def at_block(b):
    return pl.ds(pl.multiple_of(b * BLK, BLK), BLK)


def eliminate_kernel(blocks, a_ref, o_ref, *scratch):
    o_ref[...] = a_ref[...]
    eliminate(o_ref, blocks, *scratch)


def assemble_kernel(blocks, map_ref, entries_ref, first_ref, second_ref, o_ref, *scratch):
    o_ref[...] = entries_ref[...]
    for child, update in enumerate((first_ref, second_ref)):
        for i in range(4):
            for j in range(4):
                rows, columns = at_block(map_ref[child, i]), at_block(map_ref[child, j])
                part = update[i * BLK : (i + 1) * BLK, j * BLK : (j + 1) * BLK]
                o_ref[rows, columns] = o_ref[rows, columns] + part
    eliminate(o_ref, blocks, *scratch)


VMEM_SPEC = pl.BlockSpec(memory_space=pltpu.VMEM)
SMEM_SPEC = pl.BlockSpec(memory_space=pltpu.SMEM)
PARAMS = pltpu.CompilerParams(vmem_limit_bytes=60 * 1024 * 1024)


def eliminated(front, blocks):
    n = front.shape[0]
    return pl.pallas_call(
        functools.partial(eliminate_kernel, blocks),
        out_shape=jax.ShapeDtypeStruct((n, n), F32),
        in_specs=[VMEM_SPEC],
        out_specs=VMEM_SPEC,
        scratch_shapes=scratch_for(n),
        compiler_params=PARAMS,
    )(front)


def assembled_eliminated(maps, entries, first, second, blocks):
    n = entries.shape[0]
    return pl.pallas_call(
        functools.partial(assemble_kernel, blocks),
        out_shape=jax.ShapeDtypeStruct((n, n), F32),
        in_specs=[SMEM_SPEC, VMEM_SPEC, VMEM_SPEC, VMEM_SPEC],
        out_specs=VMEM_SPEC,
        scratch_shapes=scratch_for(n),
        compiler_params=PARAMS,
    )(maps, entries, first, second)


def column_of_inverse(swept, sigma, sigma_left, coupling_left, block, value, value_right, column):
    half = 4 * BLK
    whole = slice(None)

    @pl.when(block < 4)
    def _():
        put_right(value_right, whole, swept[half:, at_block(block)])
        value[...] = -dot(sigma_left[...], value_right[...])
        column[:half, :] = -swept[:half, at_block(block)]

    @pl.when(block >= 4)
    def _():
        value[...] = sigma[:, at_block(block - 4)]
        column[:half, :] = jnp.zeros((half, BLK), F32)

    lower = value[...]
    put_right(value_right, whole, lower)
    column[:half, :] = column[:half, :] - dot(coupling_left[...], value_right[...])
    column[half:, :] = lower


def back_kernel(
    map_ref, one_ref, two_ref, three_ref, o_ref, sigma, sigma_left, coupling_left, value, value_right, column, lower
):
    half = 4 * BLK
    whole = slice(None)
    for i in range(4):
        for j in range(4):
            picked = three_ref[at_block(map_ref[0, i]), at_block(map_ref[0, j])]
            sigma[i * BLK : (i + 1) * BLK, j * BLK : (j + 1) * BLK] = -picked
    put_left(sigma_left, whole, sigma[...])
    put_left(coupling_left, whole, two_ref[:half, half:])

    def step(j, carry):
        column_of_inverse(
            two_ref, sigma, sigma_left, coupling_left, map_ref[1, j], value, value_right, column
        )
        for i in range(4):
            lower[i * BLK : (i + 1) * BLK, at_block(j)] = column[at_block(map_ref[1, i]), :]
        return carry

    lax.fori_loop(0, 4, step, 0)
    put_left(sigma_left, whole, lower[...])
    put_left(coupling_left, whole, one_ref[:half, half:])
    column_of_inverse(
        one_ref, lower, sigma_left, coupling_left, map_ref[3, 0], value, value_right, column
    )
    for i in range(4):
        o_ref[i * BLK : (i + 1) * BLK, :] = column[at_block(map_ref[2, i]), :]


def back_substituted(maps, one, two, three):
    half = 4 * BLK
    return pl.pallas_call(
        back_kernel,
        out_shape=jax.ShapeDtypeStruct((half, BLK), F32),
        in_specs=[SMEM_SPEC, VMEM_SPEC, VMEM_SPEC, VMEM_SPEC],
        out_specs=VMEM_SPEC,
        scratch_shapes=[
            pltpu.VMEM((half, half), F32),
            pltpu.VMEM((half, 3 * half), BF16),
            pltpu.VMEM((half, 3 * half), BF16),
            pltpu.VMEM((half, BLK), F32),
            pltpu.VMEM((3 * half, BLK), BF16),
            pltpu.VMEM((2 * half, BLK), F32),
            pltpu.VMEM((half, half), F32),
        ],
        compiler_params=PARAMS,
    )(maps, one, two, three)


def ascended(update, bit_number, entries, maps, child_index, blocks):
    column = lax.axis_index("front")
    width = update.shape[1] // lax.axis_size("front")
    share = lax.dynamic_slice_in_dim(update, column * width, width, 1)
    partner = partner_2(share, "leaf", bit_number)
    mine_full, partner_full = side_by_side((share, partner), "front", 1, 0)
    lower_side = child_index % 2 == 0
    first = jnp.where(lower_side, mine_full, partner_full)
    second = jnp.where(lower_side, partner_full, mine_full)
    pair = lax.dynamic_slice_in_dim(maps, child_index - child_index % 2, 2, 0)
    return assembled_eliminated(pair, entries, first, second, blocks)


def body(leaf_update, front_entries1, front_entries2, front_entries3, map_leaf, map_mid, map_top):
    leaf_index = lax.axis_index("leaf")
    column = lax.axis_index("front")
    members = lax.axis_size("leaf") // 4
    low_bits = members.bit_length() - 1
    first_node = leaf_index // members
    second_node = leaf_index // (2 * members)
    order_one = SEP1 + RUP
    order_two = SEP2 + RUP
    update = gathered_copies(leaf_update, "front", 1)
    leaf_blocks = map_leaf[leaf_index]
    spread = extend(update, leaf_blocks, order_one // BLK)
    share_width = front_entries1.shape[1]
    column_share = lax.dynamic_slice_in_dim(spread, column * share_width, share_width, 1)
    entry_rows = front_entries1.shape[0]
    offset = leaf_index % members * entry_rows
    with_entries = lax.dynamic_slice_in_dim(column_share, offset, entry_rows, 0) + front_entries1
    column_share = lax.dynamic_update_slice_in_dim(column_share, with_entries, offset, 0)
    for bit_number in range(low_bits):
        halfway = column_share.shape[0] // 2
        upper_side = leaf_index >> bit_number & 1 == 1
        kept_rows = jnp.where(upper_side, column_share[halfway:], column_share[:halfway])
        sent_rows = jnp.where(upper_side, column_share[:halfway], column_share[halfway:])
        column_share = kept_rows + partner_2(sent_rows, "leaf", bit_number)
    for bit_number in reversed(range(low_bits)):
        upper_side = leaf_index >> bit_number & 1 == 1
        partner_rows = partner_2(column_share, "leaf", bit_number)
        column_share = jnp.where(
            upper_side,
            jnp.concatenate([partner_rows, column_share], axis=0),
            jnp.concatenate([column_share, partner_rows], axis=0),
        )
    front_one = lax.all_gather(column_share, "front", axis=1, tiled=True)
    one = eliminated(front_one, SEP1 // BLK)
    entries_two = lax.dynamic_slice_in_dim(front_entries2, second_node * order_two, order_two, 0)
    two = ascended(one[SEP1:, SEP1:], low_bits, entries_two, map_mid, first_node, SEP2 // BLK)
    three = ascended(
        two[SEP2:, SEP2:], low_bits + 1, front_entries3, map_top, second_node, SEP3 // BLK
    )
    own = jnp.broadcast_to(leaf_blocks[column], (4,))
    maps = jnp.stack([map_top[second_node], map_mid[first_node], leaf_blocks, own], axis=0)
    return back_substituted(maps, one, two, three)


def solution(mesh):
    in_specs = (P("leaf", "front"), P("leaf", "front"), P(), P(), P(), P(), P())
    out_specs = P("leaf", "front")
    return jax.shard_map(body, mesh=mesh, in_specs=in_specs, out_specs=out_specs, check_vma=False)
```

time: 1050 us -> 439 us (0.42); the launches traced: 1030 us -> 434 us
  other arithmetic: 573 us -> 6.65 us
  Pallas kernels: 0 us -> 195 us
  local copies, waits for them, and re-layouts: 179 us -> 29.8 us
  matrix products: 110 us -> 0 us
  waiting for transfers between devices: 106 us -> 146 us
  between operations: 25.6 us -> 13.8 us
    another operation x70 -> x1, other arithmetic: 502 us -> 0.61 us  [body(): jnp.stack([map_top[second_node], map_mid[first_node], leaf_blocks, own],...]
    pallas_call x0 -> x4, Pallas kernels: none -> 195 us  [the longest x2 137 us: assembled_eliminated(): pl.pallas_call(functools.partial(assemble_kernel, blocks), out_shape=jax....]
    another operation x69 -> x0, matrix products: 80.8 us -> none  [the longest x14 23.2 us: body(): factor_top = jnp.linalg.cholesky(front_three)]
    another operation x77 -> x1, local copies, waits for them, and re-layouts: 56.2 us -> 0.72 us  [body(): jnp.stack([map_top[second_node], map_mid[first_node], leaf_blocks, own],...]
    dot_general x11 -> x0, matrix products: 28.8 us -> none  [product(): return jnp.dot(left_side, right_side, precision=lax.Precision.HIGHEST)]
    unnamed x128 -> x7, local copies, waits for them, and re-layouts: 27.8 us -> 0.11 us
    mul x5 -> x1, local copies, waits for them, and re-layouts: 27 us -> 0.33 us  [extend(): result = picked * weight]
    mul x5 -> x1, other arithmetic: 22.5 us -> 2.09 us  [extend(): result = picked * weight]
  transfers between devices with their start and end apart: 14 -> 14, of which waited for: 13 -> 14; matrix products, arithmetic and copies ran while one was open for 6% -> 2% of each run, Pallas kernels for 0% -> 0%
where the time goes in v1:
time: 439 us; the launch traced here: 434 us
  Pallas kernels  195 us (44%)
  waiting for transfers between devices  146 us (33%)
  starting transfers between devices  42.7 us (10%)
  local copies, waits for them, and re-layouts  29.8 us (7%)
  between operations  13.8 us (3%)
  other arithmetic  6.65 us (2%)
    pallas_call x2, Pallas kernels, assembled_eliminated(): pl.pallas_call(functools.partial(assemble_kernel, blocks), out_shape=jax....  137 us
    all_gather x1, waiting for transfers between devices, body(): front_one = lax.all_gather(column_share, 'front', axis=1, tiled=True)  52 us
    all_to_all x3, waiting for transfers between devices, sent_to_all(): return lax.all_to_all(copies, axis, split_axis=0, concat_axis=0, tiled=True)  50.9 us
    pallas_call x1, Pallas kernels, eliminated(): pl.pallas_call(functools.partial(eliminate_kernel, blocks), out_shape=jax...  46.3 us
    ppermute x10, waiting for transfers between devices, partner_2(): return lax.ppermute(block, axis, route)  43 us
    ppermute x10, starting transfers between devices, partner_2(): return lax.ppermute(block, axis, route)  30.5 us
    all_to_all x3, starting transfers between devices, sent_to_all(): return lax.all_to_all(copies, axis, split_axis=0, concat_axis=0, tiled=True)  12.2 us
    pallas_call x1, Pallas kernels, back_substituted(): pl.pallas_call(back_kernel, out_shape=jax.ShapeDtypeStruct((half, BLK), F...  11.6 us
  transfers between devices with their start and end apart: 14, of which 14 were waited for; matrix products, arithmetic and copies ran while one was open for 2% of the time, Pallas kernels for 0%

profile of v1, /device:TPU:1, one launch (start us, length us, event | category | flops | bytes accessed | tf_op | source)
XLA Modules:
  0.0 433.5 jit_solution(8824360182844400646)
XLA Ops:
  6.5 2.0 broadcast_in_dim.41
  8.5 5.0 %all-to-all-start = ((f32[4,512,128]{2,1,0:T(8,128)}), f32[4,512,128]{2,1,0:T(8,128)S(1)}, u32[]{:S(2)}, u32[]{:S(2)}) async-start(f32[4,512,128]{2,1,0:T(8,128)} %broadcast_in_dim.41), calls=%async_computation | async-start | bytes 2097152 | tf_op jit(solution)/shard_map/all_to_all | solution.py:35
  14.7 12.3 %all-to-all-done = f32[4,512,128]{2,1,0:T(8,128)S(1)} async-done(((f32[4,512,128]{2,1,0:T(8,128)}), f32[4,512,128]{2,1,0:T(8,128)S(1)}, u32[]{:S(2)}, u32[]{:S(2)}) %all-to-all-start) | async-done | bytes 1048608 | tf_op jit(solution)/shard_map/all_to_all | solution.py:35
  27.1 2.0 gather_fusion
  29.2 1.9 broadcast_select_fusion
  31.0 2.8 gather_fusion.1
  33.8 4.6 %copy.23 = f32[8,128,8,128]{3,2,1,0:T(8,128)S(1)} copy(f32[8,128,8,128]{3,1,0,2:T(8,128)} %bitcast.46) | data formatting | bytes 8388608 | tf_op jit(solution)/shard_map/jit(_take)/gather | solution.py:71
  38.7 2.1 bitcast_multiply_fusion
  41.1 2.6 collective-permute-start
  46.8 6.3 %collective-permute-done.1 = f32[256,256]{1,0:T(8,128)S(1)} collective-permute-done((f32[256,256]{1,0:T(8,128)S(1)}, f32[256,256]{1,0:T(8,128)S(1)}, u32[]{:S(2)}, u32[]{:S(2)}) %collective-permute-start.1) | collective-permute-done | bytes 262176 | tf_op jit(solution)/shard_map/ppermute | solution.py:24
  53.1 2.8 collective-permute-start.2
  55.9 2.6 collective-permute-done.2
  58.6 1.7 collective-permute-start.3
  63.5 1.8 collective-permute-done.4
  65.3 2.8 collective-permute-start.5
  68.2 2.6 collective-permute-done.5
  72.1 5.4 %collective-permute-done.6 = f32[256,256]{1,0:T(8,128)S(1)} collective-permute-done((f32[256,256]{1,0:T(8,128)S(1)}, f32[256,256]{1,0:T(8,128)S(1)}, u32[]{:S(2)}, u32[]{:S(2)}) %collective-permute-start.6) | collective-permute-done | bytes 262176 | tf_op jit(solution)/shard_map/ppermute | solution.py:24
  77.5 6.6 %collective-permute-start.7 = (f32[512,256]{1,0:T(8,128)S(1)}, f32[512,256]{1,0:T(8,128)S(1)}, u32[]{:S(2)}, u32[]{:S(2)}) collective-permute-start(f32[512,256]{1,0:T(8,128)S(1)} %maximum_select_fusion.1), channel_id=1, source_target_pairs={{0,4},{4,0},{8,12},{12,8},{16,20},{20,16},{24,28},{28,24},{32,36},... | collective-permute-start | bytes 1572872 | tf_op jit(solution)/shard_map/ppermute | solution.py:24
  86.8 52.0 %all-gather.2.cloned.1.call-done.a_ref = f32[1024,1024]{1,0:T(8,128)} async-done(((f32[1024,256]{1,0:T(8,128)}), f32[1024,1024]{1,0:T(8,128)}) %all-gather.2.cloned.1.call-update) | async-done | bytes 4194320 | tf_op jit(solution)/shard_map/all_gather | solution.py:380
  138.8 46.3 %shard_map.73.one_ref = f32[1024,1024]{1,0:T(8,128)} custom-call(f32[1024,1024]{1,0:T(8,128)} %all-gather.2.cloned.1.call-done.a_ref), custom_call_target="tpu_custom_call" | custom-call | tf_op jit(solution)/shard_map/pallas_call | solution.py:242
  186.5 2.3 collective-permute-start.8
  188.8 11.5 %collective-permute-done.8 = f32[512,128]{1,0:T(8,128)S(1)} collective-permute-done((f32[512,128]{1,0:T(8,128)S(1)}, f32[512,128]{1,0:T(8,128)S(1)}, u32[]{:S(2)}, u32[]{:S(2)}) %collective-permute-start.8) | collective-permute-done | bytes 262176 | tf_op jit(solution)/shard_map/ppermute | solution.py:24
  201.9 3.6 all-to-all-start.1
  206.1 4.7 %constant_dynamic-slice_fusion.2.entries_ref = f32[1024,1024]{1,0:T(8,128)} fusion(f32[2048,1024]{1,0:T(8,128)} %param.9, s32[]{:T(128)S(6)} %select_n.234), kind=kLoop, calls=%fused_computation.33 | loop fusion | bytes 8388612 | tf_op jit(solution)/shard_map/dynamic_slice | solution.py:382
  210.9 19.5 %all-to-all-done.1 = f32[4,1024,128]{2,1,0:T(8,128)S(1)} async-done(((f32[4,1024,128]{2,1,0:T(8,128)}), f32[4,1024,128]{2,1,0:T(8,128)S(1)}, u32[]{:S(2)}, u32[]{:S(2)}) %all-to-all-start.1) | async-done | bytes 2097184 | tf_op jit(solution)/shard_map/all_to_all | solution.py:35
  232.2 47.5 %shard_map.74.two_ref = f32[1024,1024]{1,0:T(8,128)} custom-call(s32[2,4]{1,0:T(2,128)} %constant_dynamic-slice_fusion.3.map_ref, f32[1024,1024]{1,0:T(8,128)} %constant_dynamic-slice_fusion.2.entries_ref, f32[512,512]{1,0:T(8,128)} %get-tuple-element.14.first_ref, f32[512,512]{1,0:T(8,128)} %get-tuple-element.13.second_ref), custom_call_target="tpu_custom_call" | custom-call | tf_op jit(solution)/shard_map/pallas_call | solution.py:254
  281.0 7.4 %collective-permute-start.9 = (f32[512,128]{1,0:T(8,128)S(1)}, f32[512,128]{1,0:T(8,128)S(1)}, u32[]{:S(2)}, u32[]{:S(2)}) collective-permute-start(f32[512,128]{1,0:T(8,128)S(1)} %constant_dynamic-slice_fusion), channel_id=1, source_target_pairs={{0,128},{128,0},{4,132},{132,4},{8,136},{136,8},{12,140},{140,12},... | collective-permute-start | bytes 786440 | tf_op jit(solution)/shard_map/ppermute | solution.py:24
  288.3 8.2 %collective-permute-done.9 = f32[512,128]{1,0:T(8,128)S(1)} collective-permute-done((f32[512,128]{1,0:T(8,128)S(1)}, f32[512,128]{1,0:T(8,128)S(1)}, u32[]{:S(2)}, u32[]{:S(2)}) %collective-permute-start.9) | collective-permute-done | bytes 262176 | tf_op jit(solution)/shard_map/ppermute | solution.py:24
  298.1 3.6 all-to-all-start.2
  304.3 19.0 %all-to-all-done.2 = f32[4,1024,128]{2,1,0:T(8,128)S(1)} async-done(((f32[4,1024,128]{2,1,0:T(8,128)}), f32[4,1024,128]{2,1,0:T(8,128)S(1)}, u32[]{:S(2)}, u32[]{:S(2)}) %all-to-all-start.2) | async-done | bytes 2097184 | tf_op jit(solution)/shard_map/all_to_all | solution.py:35
  325.8 89.4 %shard_map.75.three_ref = f32[1024,1024]{1,0:T(8,128)} custom-call(s32[2,4]{1,0:T(2,128)} %map_ref, f32[1024,1024]{1,0:T(8,128)} %entries_ref.1, f32[512,512]{1,0:T(8,128)} %bitcast.51, f32[512,512]{1,0:T(8,128)} %bitcast.50), custom_call_target="tpu_custom_call" | custom-call | tf_op jit(solution)/shard_map/pallas_call | solution.py:254
  415.1 11.6 %shard_map.76 = f32[512,128]{1,0:T(8,128)} custom-call(s32[4,4]{1,0:T(4,128)} %add_add_fusion.map_ref, f32[1024,1024]{1,0:T(8,128)} %shard_map.73.one_ref, f32[1024,1024]{1,0:T(8,128)} %shard_map.74.two_ref, f32[1024,1024]{1,0:T(8,128)} %shard_map.75.three_ref), custom_call_target="tpu_custom_call" | custom-call | tf_op jit(solution)/shard_map/pallas_call | solution.py:317
  (57 shorter events, 25.3 us)
Async XLA Ops:
  8.5 18.5 %all-to-all-start = ((f32[4,512,128]{2,1,0:T(8,128)}), f32[4,512,128]{2,1,0:T(8,128)S(1)}, u32[]{:S(2)}, u32[]{:S(2)}) async-start(f32[4,512,128]{2,1,0:T(8,128)} %broadcast_in_dim.41), calls=%async_computation | async-start | bytes 2097152 | tf_op jit(solution)/shard_map/all_to_all | solution.py:35
  13.5 125.3 %all-gather.2.cloned.1.call-start = ((), (), s32[]{:S(2)}) async-start(), calls=%async_computation.3 | async-start | bytes 5242880 | tf_op jit(solution)/shard_map/all_gather | solution.py:380
  38.7 2.2 copy-start
  41.1 4.2 collective-permute-start
  45.5 7.6 %collective-permute-start.1 = (f32[256,256]{1,0:T(8,128)S(1)}, f32[256,256]{1,0:T(8,128)S(1)}, u32[]{:S(2)}, u32[]{:S(2)}) collective-permute-start(f32[256,256]{1,0:T(8,128)S(1)} %slice_select_fusion.1), channel_id=1, source_target_pairs={{0,8},{8,0},{4,12},{12,4},{16,24},{24,16},{20,28},{28,20},{32,40},... | collective-permute-start | bytes 786440 | tf_op jit(solution)/shard_map/ppermute | solution.py:24
  53.1 5.4 %collective-permute-start.2 = (f32[128,256]{1,0:T(8,128)S(1)}, f32[128,256]{1,0:T(8,128)S(1)}, u32[]{:S(2)}, u32[]{:S(2)}) collective-permute-start(f32[128,256]{1,0:T(8,128)S(1)} %slice_select_fusion.2), channel_id=1, source_target_pairs={{0,16},{16,0},{4,20},{20,4},{8,24},{24,8},{12,28},{28,12},{32,48},... | collective-permute-start | bytes 393224 | tf_op jit(solution)/shard_map/ppermute | solution.py:24
  58.6 3.4 collective-permute-start.3
  62.0 3.3 collective-permute-start.4
  65.3 5.4 %collective-permute-start.5 = (f32[128,256]{1,0:T(8,128)S(1)}, f32[128,256]{1,0:T(8,128)S(1)}, u32[]{:S(2)}, u32[]{:S(2)}) collective-permute-start(f32[128,256]{1,0:T(8,128)S(1)} %maximum_select_fusion.3), channel_id=1, source_target_pairs={{0,16},{16,0},{4,20},{20,4},{8,24},{24,8},{12,28},{28,12},{32,48},... | collective-permute-start | bytes 393224 | tf_op jit(solution)/shard_map/ppermute | solution.py:24
  70.8 6.7 %collective-permute-start.6 = (f32[256,256]{1,0:T(8,128)S(1)}, f32[256,256]{1,0:T(8,128)S(1)}, u32[]{:S(2)}, u32[]{:S(2)}) collective-permute-start(f32[256,256]{1,0:T(8,128)S(1)} %maximum_select_fusion.2), channel_id=1, source_target_pairs={{0,8},{8,0},{4,12},{12,4},{16,24},{24,16},{20,28},{28,20},{32,40},... | collective-permute-start | bytes 786440 | tf_op jit(solution)/shard_map/ppermute | solution.py:24
  77.5 8.1 %collective-permute-start.7 = (f32[512,256]{1,0:T(8,128)S(1)}, f32[512,256]{1,0:T(8,128)S(1)}, u32[]{:S(2)}, u32[]{:S(2)}) collective-permute-start(f32[512,256]{1,0:T(8,128)S(1)} %maximum_select_fusion.1), channel_id=1, source_target_pairs={{0,4},{4,0},{8,12},{12,8},{16,20},{20,16},{24,28},{28,24},{32,36},... | collective-permute-start | bytes 1572872 | tf_op jit(solution)/shard_map/ppermute | solution.py:24
  186.4 19.1 %copy-start.2 = (s32[4,4]{1,0:T(4,128)S(1)}, s32[4,4]{1,0:T(4,128)}, u32[]{:S(2)}) copy-start(s32[4,4]{1,0:T(4,128)} %param.12) | copy-start | bytes 196
  186.5 13.8 %collective-permute-start.8 = (f32[512,128]{1,0:T(8,128)S(1)}, f32[512,128]{1,0:T(8,128)S(1)}, u32[]{:S(2)}, u32[]{:S(2)}) collective-permute-start(f32[512,128]{1,0:T(8,128)S(1)} %constant_dynamic-slice_fusion.1), channel_id=1, source_target_pairs={{0,64},{64,0},{4,68},{68,4},{8,72},{72,8},{12,76},{76,12},{16,80},... | collective-permute-start | bytes 786440 | tf_op jit(solution)/shard_map/ppermute | solution.py:24
  201.9 28.5 %all-to-all-start.1 = ((f32[4,1024,128]{2,1,0:T(8,128)}), f32[4,1024,128]{2,1,0:T(8,128)S(1)}, u32[]{:S(2)}, u32[]{:S(2)}) async-start(f32[4,1024,128]{2,1,0:T(8,128)} %broadcast_in_dim.44), calls=%async_computation.1 | async-start | bytes 4194304 | tf_op jit(solution)/shard_map/all_to_all | solution.py:35
  280.9 22.8 %copy-start.1 = (s32[2,4]{1,0:T(2,128)S(1)}, s32[2,4]{1,0:T(2,128)}, u32[]{:S(2)}) copy-start(s32[2,4]{1,0:T(2,128)} %map_ref) | copy-start | bytes 100
  281.0 15.5 %collective-permute-start.9 = (f32[512,128]{1,0:T(8,128)S(1)}, f32[512,128]{1,0:T(8,128)S(1)}, u32[]{:S(2)}, u32[]{:S(2)}) collective-permute-start(f32[512,128]{1,0:T(8,128)S(1)} %constant_dynamic-slice_fusion), channel_id=1, source_target_pairs={{0,128},{128,0},{4,132},{132,4},{8,136},{136,8},{12,140},{140,12},... | collective-permute-start | bytes 786440 | tf_op jit(solution)/shard_map/ppermute | solution.py:24
  298.1 25.2 %all-to-all-start.2 = ((f32[4,1024,128]{2,1,0:T(8,128)}), f32[4,1024,128]{2,1,0:T(8,128)S(1)}, u32[]{:S(2)}, u32[]{:S(2)}) async-start(f32[4,1024,128]{2,1,0:T(8,128)} %broadcast_in_dim.45), calls=%async_computation.2 | async-start | bytes 4194304 | tf_op jit(solution)/shard_map/all_to_all | solution.py:35
Sparse Core Ops, SparseCore 0:
  86.9 51.8 all-gather.1

commit v2 on v1

--- a/solution.py
+++ b/solution.py
@@ -12,66 +12,6 @@
 SEP2 = 512
 SEP3 = 1024
 RUP = 512
-
-
-def partner_2(block, axis, distance):
-    count = lax.axis_size(axis)
-    route = []
-    for low in range(count):
-        high = low | 1 << distance
-        if high != low and high < count:
-            route += [(low, high), (high, low)]
-    return lax.ppermute(block, axis, route)
-
-
-def laid_out(tiles, dim):
-    dims = list(tiles.shape[1:])
-    dims[dim] *= tiles.shape[0]
-    return jnp.moveaxis(tiles, 0, dim).reshape(dims)
-
-
-def sent_to_all(shard, axis):
-    copies = jnp.broadcast_to(shard, (lax.axis_size(axis), *shard.shape))
-    return lax.all_to_all(copies, axis, split_axis=0, concat_axis=0, tiled=True)
-
-
-def gathered_copies(shard, axis, dim):
-    return laid_out(sent_to_all(shard, axis), dim)
-
-
-def side_by_side(arrays, axis, dim, along):
-    ends, at = ([], 0)
-    for a in arrays[:-1]:
-        at += a.shape[along]
-        ends.append(at)
-    both = jnp.concatenate(arrays, axis=along)
-    return tuple(jnp.split(gathered_copies(both, axis, dim), ends, axis=along))
-
-
-def product(left_side, right_side):
-    return jnp.dot(left_side, right_side, precision=lax.Precision.HIGHEST)
-
-
-def placement(block_list, parent_blocks):
-    child_blocks = block_list.shape[0]
-    hits = (block_list[:, None] == jnp.arange(parent_blocks, dtype=jnp.int32)[None, :]).astype(
-        jnp.int32
-    )
-    source = jnp.sum(hits * jnp.arange(child_blocks, dtype=jnp.int32)[:, None], axis=0)
-    present = jnp.sum(hits, axis=0).astype(jnp.float32)
-    return (source, present)
-
-
-def extend(update, block_list, parent_blocks):
-    child_blocks = block_list.shape[0]
-    block_rows = update.shape[0] // child_blocks
-    source, present = placement(block_list, parent_blocks)
-    blocked = update.reshape(child_blocks, block_rows, child_blocks, block_rows)
-    picked_rows = jnp.take(blocked, source, axis=0)
-    picked = jnp.take(picked_rows, source, axis=2)
-    weight = present[:, None, None, None] * present[None, None, :, None]
-    result = picked * weight
-    return result.reshape(parent_blocks * block_rows, parent_blocks * block_rows)
 
 
 F32, BF16 = jnp.float32, jnp.bfloat16
@@ -216,20 +156,308 @@
     return pl.ds(pl.multiple_of(b * BLK, BLK), BLK)
 
 
-def eliminate_kernel(blocks, a_ref, o_ref, *scratch):
-    o_ref[...] = a_ref[...]
+LOWER = [(a, b) for y in range(4) for a in (y, 7 - y) for b in range(a + 1)]
+SHARE = [(i, j) for i in range(4) for j in range(i + 1)]
+
+
+def pack_update(o, tri):
+    for t, (i, j) in enumerate(SHARE):
+        tri[t * BLK : (t + 1) * BLK, :] = o[
+            SEP1 + i * BLK : SEP1 + (i + 1) * BLK, SEP1 + j * BLK : SEP1 + (j + 1) * BLK
+        ]
+
+
+def first_kernel(blocks, lower_ref, o_ref, tri_ref, *scratch):
+    for t, (a, b) in enumerate(LOWER):
+        part = lower_ref[t]
+        o_ref[a * BLK : (a + 1) * BLK, b * BLK : (b + 1) * BLK] = part
+        if a != b:
+            o_ref[b * BLK : (b + 1) * BLK, a * BLK : (a + 1) * BLK] = part.T
     eliminate(o_ref, blocks, *scratch)
-
-
-def assemble_kernel(blocks, map_ref, entries_ref, first_ref, second_ref, o_ref, *scratch):
-    o_ref[...] = entries_ref[...]
-    for child, update in enumerate((first_ref, second_ref)):
-        for i in range(4):
-            for j in range(4):
-                rows, columns = at_block(map_ref[child, i]), at_block(map_ref[child, j])
-                part = update[i * BLK : (i + 1) * BLK, j * BLK : (j + 1) * BLK]
-                o_ref[rows, columns] = o_ref[rows, columns] + part
+    pack_update(o_ref, tri_ref)
+
+
+def add_child(o_ref, update, maps, child):
+    for t, (i, j) in enumerate(SHARE):
+        rows, columns = at_block(maps[child, i]), at_block(maps[child, j])
+        part = update[t * BLK : (t + 1) * BLK, :]
+        o_ref[rows, columns] = o_ref[rows, columns] + part
+        if i != j:
+            o_ref[columns, rows] = o_ref[columns, rows] + part.T
+
+
+def next_kernel(blocks, packs, map_ref, entries_ref, mine_ref, other_ref, o_ref, *rest):
+    tri_ref, rest = (rest[0], rest[1:]) if packs else (None, rest)
+    copied, scratch = rest[0], rest[1:]
+    n = o_ref.shape[0]
+    start = pl.multiple_of(map_ref[2, 0] * n, 8)
+    fetch = pltpu.make_async_copy(entries_ref.at[pl.ds(start, n), :], o_ref, copied)
+    fetch.start()
+    fetch.wait()
+    add_child(o_ref, mine_ref, map_ref, 0)
+    add_child(o_ref, other_ref, map_ref, 1)
     eliminate(o_ref, blocks, *scratch)
+    if packs:
+        pack_update(o_ref, tri_ref)
+
+
+def remote(source, target, sent, received, leaf, front):
+    return pltpu.make_async_remote_copy(
+        src_ref=source,
+        dst_ref=target,
+        send_sem=sent,
+        recv_sem=received,
+        device_id=(leaf, front),
+        device_id_type=pl.DeviceIdType.MESH,
+    )
+
+
+def greet(devices):
+    barrier = pltpu.get_barrier_semaphore()
+    for device in devices:
+        pl.semaphore_signal(
+            barrier, inc=1, device_id=device, device_id_type=pl.DeviceIdType.MESH
+        )
+    pl.semaphore_wait(barrier, len(devices))
+
+
+def exchange_kernel(distance, tri_ref, o_ref, sent, got):
+    leaf, y = lax.axis_index("leaf"), lax.axis_index("front")
+    core, x = leaf % 2, (leaf // 2) % 4
+    z = leaf // 8
+    sibling = leaf + distance * (1 - 2 * ((leaf // distance) % 2))
+    other_core = leaf + 1 - 2 * core
+    rows = tri_ref.shape[0] // 32
+
+    def in_x(d):
+        return z * 8 + ((x + d) % 4) * 2 + core
+
+    greet(
+        [(sibling, y), (other_core, y)]
+        + [(leaf, (y + d) % 4) for d in (1, 2, 3)]
+        + [(in_x(d), y) for d in (1, 2, 3)]
+    )
+
+    def share(c, xx, yy):
+        return pl.ds(pl.multiple_of(((c * 4 + xx) * 4 + yy) * rows, 8), rows)
+
+    def row(c, xx):
+        return pl.ds(pl.multiple_of((c * 4 + xx) * 4 * rows, 8), 4 * rows)
+
+    mine = share(core, x, y)
+    across = remote(tri_ref.at[mine], o_ref.at[mine], sent.at[0], got.at[0], sibling, y)
+    across.start()
+    across.wait_recv()
+    spread = [
+        remote(o_ref.at[mine], o_ref.at[mine], sent.at[d], got.at[d], leaf, (y + d) % 4)
+        for d in (1, 2, 3)
+    ]
+    for copy in spread:
+        copy.start()
+    for copy in spread:
+        copy.wait_recv()
+    whole = row(core, x)
+    wide = [
+        remote(o_ref.at[whole], o_ref.at[whole], sent.at[3 + d], got.at[3 + d], in_x(d), y)
+        for d in (1, 2, 3)
+    ]
+    for copy in wide:
+        copy.start()
+    last = []
+    for d in (0, 3, 1, 2):
+        if d:
+            wide[d - 1].wait_recv()
+        piece = row(core, (x - d + 4) % 4)
+        copy = remote(o_ref.at[piece], o_ref.at[piece], sent.at[7 + d], got.at[7 + d], other_core, y)
+        copy.start()
+        last.append(copy)
+    for copy in last:
+        copy.wait_recv()
+    for copy in [across] + spread + wide + last:
+        copy.wait_send()
+
+
+def gather_kernel(
+    table_ref, leaf_ref, entries_ref, o_ref,
+    met, partial, halves_in, own_entries,
+    keep, sent, got, sent_e, got_e, sent_y, got_y, sent_x, got_x, sent_c, got_c,
+):
+    leaf, y = lax.axis_index("leaf"), lax.axis_index("front")
+    m = leaf % 16
+    base = leaf - m
+    core, x, z = m % 2, (m // 2) % 4, m // 8
+    me = m * 4 + y
+    barrier = pltpu.get_barrier_semaphore()
+
+    def meet(d, carry):
+        other = (me + d) % 64
+        pl.semaphore_signal(
+            barrier,
+            inc=1,
+            device_id=(base + other // 4, other % 4),
+            device_id_type=pl.DeviceIdType.MESH,
+        )
+        return carry
+
+    lax.fori_loop(1, 64, meet, 0)
+    met[:, 4] = jnp.zeros((16, 8, BLK), F32)
+    pl.semaphore_wait(barrier, 63)
+
+    kept = pltpu.make_async_copy(leaf_ref.at[:, m], met.at[m, 0:4], keep.at[0])
+    kept.start()
+    members = []
+    for d in range(1, 16):
+        to = (m + d) % 16
+        members.append(
+            remote(leaf_ref.at[:, to], met.at[m, 0:4], sent.at[d], got.at[d], base + to, y)
+        )
+        members[-1].start()
+    a, half = m // 2, m % 2
+    high = a // 4
+    target_y = a + high * (7 - 2 * a)
+    wide = pl.ds(pl.multiple_of(y * 256, 256), 256)
+    for g in range(8):
+        to = half * 8 + g
+        source = entries_ref.at[pl.ds(8 * g, 8), :]
+        target = own_entries.at[high, :, wide]
+        stays = jnp.logical_and(to == m, target_y == y)
+
+        @pl.when(stays)
+        def _():
+            copy = pltpu.make_async_copy(source, target, got_e.at[high, y])
+            copy.start()
+
+        @pl.when(jnp.logical_not(stays))
+        def _():
+            remote(
+                source, target, sent_e.at[g], got_e.at[high, y], base + to, target_y
+            ).start()
+
+    kept.wait()
+    for copy in members:
+        copy.wait_recv()
+
+    def sum_block(t, carry):
+        total = met[table_ref[t, 0] // 5, table_ref[t, 0] % 5]
+        for s in range(1, 16):
+            index = table_ref[t, s]
+            total = total + met[index // 5, index % 5]
+        partial[t] = total
+        return carry
+
+    lax.fori_loop(0, 36, sum_block, 0)
+    to_sum = []
+    for d in (1, 2, 3):
+        to = (y + d) % 4
+        to_sum.append(
+            remote(
+                partial.at[pl.ds(9 * to, 9)], halves_in.at[d - 1],
+                sent_y.at[d - 1], got_y.at[d - 1], leaf, to,
+            )
+        )
+        to_sum[-1].start()
+    for h in range(2):
+        for c in range(4):
+            pltpu.make_async_copy(
+                entries_ref.at[pl.ds(0, 8), :],
+                own_entries.at[h, :, pl.ds(c * 256, 256)],
+                got_e.at[h, c],
+            ).wait()
+    for copy in to_sum:
+        copy.wait_recv()
+    rows = pl.ds(pl.multiple_of(m * 8, 8), 8)
+    for t in range(9):
+        second = (t + 8 - y) // 9
+        b = t - second * (y + 1)
+        entry = own_entries[second, :, pl.ds(pl.multiple_of(b * BLK, BLK), BLK)]
+        value = partial[9 * y + t] + halves_in[0, t] + halves_in[1, t] + halves_in[2, t]
+        o_ref[9 * y + t, rows, :] = value + entry
+    spread = []
+    own = o_ref.at[pl.ds(9 * y, 9), rows, :]
+    for d in (1, 2, 3):
+        spread.append(
+            remote(own, own, sent_y.at[2 + d], got_y.at[2 + d], leaf, (y + d) % 4)
+        )
+        spread[-1].start()
+    for copy in spread:
+        copy.wait_recv()
+
+    other_z = base + (m + 8) % 16
+    other_core = base + m + 1 - 2 * core
+
+    def piece(xx, zz, part):
+        slot = pl.ds(pl.multiple_of((zz * 8 + xx * 2 + core) * 8, 8), 8)
+        return o_ref.at[18 * part : 18 * part + 18, slot, :]
+
+    def step_x(xx, zz, part, direction, slot):
+        to = base + z * 8 + ((x + direction + 4) % 4) * 2 + core
+        ref = piece(xx, zz, part)
+        return remote(ref, ref, sent_x.at[slot], got_x.at[slot], to, y)
+
+    def to_core(xx, zz, part, slot):
+        ref = piece(xx, zz, part)
+        return remote(ref, ref, sent_c.at[slot], got_c.at[slot], other_core, y)
+
+    started = []
+
+    def begin(copy):
+        copy.start()
+        started.append(copy)
+        return copy
+
+    left, right, far = (x + 3) % 4, (x + 1) % 4, (x + 2) % 4
+    other = 1 - z
+    over_z = []
+    for part in range(2):
+        ref = piece(x, z, part)
+        over_z.append(begin(remote(ref, ref, sent_y.at[6 + part], got_y.at[6 + part], other_z, y)))
+    passes, cores = [], []
+    for stage, zz in ((0, z), (1, other)):
+        if stage:
+            for copy in over_z:
+                copy.wait_recv()
+        s = 6 * stage
+        passes.append(
+            [begin(step_x(x, zz, part, 1, s + part)) for part in range(2)]
+            + [begin(step_x(x, zz, part, -1, s + 2 + part)) for part in range(2)]
+        )
+        for part in range(2):
+            cores.append(begin(to_core(x, zz, part, 8 * stage + part)))
+    for stage, zz in ((0, z), (1, other)):
+        s = 6 * stage
+        c = 8 * stage
+        moves = passes[stage]
+        moves[0].wait_recv()
+        relay_right = begin(step_x(left, zz, 0, 1, s + 4))
+        cores.append(begin(to_core(left, zz, 0, c + 2)))
+        moves[3].wait_recv()
+        relay_left = begin(step_x(right, zz, 1, -1, s + 5))
+        cores.append(begin(to_core(right, zz, 1, c + 3)))
+        moves[1].wait_recv()
+        cores.append(begin(to_core(left, zz, 1, c + 4)))
+        moves[2].wait_recv()
+        cores.append(begin(to_core(right, zz, 0, c + 5)))
+        passes.append((relay_right, relay_left))
+    for stage, zz in ((0, z), (1, other)):
+        relay_right, relay_left = passes[2 + stage]
+        c = 8 * stage
+        relay_right.wait_recv()
+        cores.append(begin(to_core(far, zz, 0, c + 6)))
+        relay_left.wait_recv()
+        cores.append(begin(to_core(far, zz, 1, c + 7)))
+    for copy in cores:
+        copy.wait_recv()
+    for copy in members + to_sum + spread + started:
+        copy.wait_send()
+    for g in range(8):
+        to = half * 8 + g
+
+        @pl.when(jnp.logical_not(jnp.logical_and(to == m, target_y == y)))
+        def _():
+            remote(
+                entries_ref.at[pl.ds(8 * g, 8), :], own_entries.at[high, :, wide],
+                sent_e.at[g], got_e.at[high, y], base + to, target_y,
+            ).wait_send()
 
 
 VMEM_SPEC = pl.BlockSpec(memory_space=pltpu.VMEM)
@@ -237,28 +465,69 @@
 PARAMS = pltpu.CompilerParams(vmem_limit_bytes=60 * 1024 * 1024)
 
 
-def eliminated(front, blocks):
-    n = front.shape[0]
+def gathered(table, leaf_update, entries):
+    dma = pltpu.SemaphoreType.DMA
     return pl.pallas_call(
-        functools.partial(eliminate_kernel, blocks),
-        out_shape=jax.ShapeDtypeStruct((n, n), F32),
+        gather_kernel,
+        out_shape=jax.ShapeDtypeStruct((36, BLK, BLK), F32),
+        in_specs=[SMEM_SPEC, VMEM_SPEC, VMEM_SPEC],
+        out_specs=VMEM_SPEC,
+        scratch_shapes=[
+            pltpu.VMEM((16, 5, 8, BLK), F32),
+            pltpu.VMEM((36, 8, BLK), F32),
+            pltpu.VMEM((3, 9, 8, BLK), F32),
+            pltpu.VMEM((2, 8, 1024), F32),
+            dma((1,)), dma((16,)), dma((16,)), dma((8,)), dma((2, 4)), dma((8,)), dma((8,)),
+            dma((12,)), dma((12,)), dma((16,)), dma((16,)),
+        ],
+        compiler_params=pltpu.CompilerParams(
+            vmem_limit_bytes=32 * 1024 * 1024, collective_id=0, has_side_effects=True
+        ),
+    )(table, leaf_update.reshape(4, 16, 8, BLK), entries)
+
+
+def exchanged(tri, distance, collective_id):
+    dma = pltpu.SemaphoreType.DMA
+    return pl.pallas_call(
+        functools.partial(exchange_kernel, distance),
+        out_shape=jax.ShapeDtypeStruct(tri.shape, F32),
         in_specs=[VMEM_SPEC],
         out_specs=VMEM_SPEC,
+        scratch_shapes=[dma((11,)), dma((11,))],
+        compiler_params=pltpu.CompilerParams(
+            vmem_limit_bytes=16 * 1024 * 1024, collective_id=collective_id, has_side_effects=True
+        ),
+    )(tri)
+
+
+def first_eliminated(lower, blocks):
+    n = 8 * BLK
+    return pl.pallas_call(
+        functools.partial(first_kernel, blocks),
+        out_shape=(
+            jax.ShapeDtypeStruct((n, n), F32),
+            jax.ShapeDtypeStruct((10 * BLK, BLK), F32),
+        ),
+        in_specs=[VMEM_SPEC],
+        out_specs=(VMEM_SPEC, VMEM_SPEC),
         scratch_shapes=scratch_for(n),
         compiler_params=PARAMS,
-    )(front)
-
-
-def assembled_eliminated(maps, entries, first, second, blocks):
-    n = entries.shape[0]
+    )(lower)
+
+
+def next_eliminated(maps, entries, mine, other, blocks, packs):
+    n = 8 * BLK
+    out = [jax.ShapeDtypeStruct((n, n), F32)]
+    if packs:
+        out.append(jax.ShapeDtypeStruct((10 * BLK, BLK), F32))
     return pl.pallas_call(
-        functools.partial(assemble_kernel, blocks),
-        out_shape=jax.ShapeDtypeStruct((n, n), F32),
-        in_specs=[SMEM_SPEC, VMEM_SPEC, VMEM_SPEC, VMEM_SPEC],
-        out_specs=VMEM_SPEC,
-        scratch_shapes=scratch_for(n),
+        functools.partial(next_kernel, blocks, packs),
+        out_shape=tuple(out),
+        in_specs=[SMEM_SPEC, pl.BlockSpec(memory_space=pl.ANY), VMEM_SPEC, VMEM_SPEC],
+        out_specs=tuple([VMEM_SPEC] * len(out)),
+        scratch_shapes=[pltpu.SemaphoreType.DMA] + scratch_for(n),
         compiler_params=PARAMS,
-    )(maps, entries, first, second)
+    )(maps, entries, mine, other)
 
 
 def column_of_inverse(swept, sigma, sigma_left, coupling_left, block, value, value_right, column):
@@ -332,58 +601,37 @@
     )(maps, one, two, three)
 
 
-def ascended(update, bit_number, entries, maps, child_index, blocks):
-    column = lax.axis_index("front")
-    width = update.shape[1] // lax.axis_size("front")
-    share = lax.dynamic_slice_in_dim(update, column * width, width, 1)
-    partner = partner_2(share, "leaf", bit_number)
-    mine_full, partner_full = side_by_side((share, partner), "front", 1, 0)
-    lower_side = child_index % 2 == 0
-    first = jnp.where(lower_side, mine_full, partner_full)
-    second = jnp.where(lower_side, partner_full, mine_full)
-    pair = lax.dynamic_slice_in_dim(maps, child_index - child_index % 2, 2, 0)
-    return assembled_eliminated(pair, entries, first, second, blocks)
+def with_place(maps, child, place):
+    sibling = child + 1 - 2 * (child % 2)
+    return jnp.stack([maps[child], maps[sibling], jnp.broadcast_to(place, (4,))], axis=0)
 
 
 def body(leaf_update, front_entries1, front_entries2, front_entries3, map_leaf, map_mid, map_top):
     leaf_index = lax.axis_index("leaf")
     column = lax.axis_index("front")
     members = lax.axis_size("leaf") // 4
-    low_bits = members.bit_length() - 1
     first_node = leaf_index // members
     second_node = leaf_index // (2 * members)
-    order_one = SEP1 + RUP
-    order_two = SEP2 + RUP
-    update = gathered_copies(leaf_update, "front", 1)
+    below = lax.dynamic_slice_in_dim(map_leaf, first_node * members, members, 0)
+    rows = jnp.array([a for a, _ in LOWER], jnp.int32)[:, None]
+    columns = jnp.array([b for _, b in LOWER], jnp.int32)[:, None]
+    found = jnp.full((len(LOWER), members), 4, jnp.int32)
+    for i in range(4):
+        found = jnp.where(rows == below[:, i][None, :], i, found)
+    landing = lax.dynamic_index_in_dim(below, column, 1, keepdims=False)
+    found = jnp.where(columns == landing[None, :], found, 4)
+    table = found + 5 * jnp.arange(members, dtype=jnp.int32)[None, :]
+    lower = gathered(table, leaf_update, front_entries1)
+    one, update = first_eliminated(lower, SEP1 // BLK)
+    other = exchanged(update, members, 1)
+    two, update = next_eliminated(
+        with_place(map_mid, first_node, second_node), front_entries2, update, other, SEP2 // BLK, True
+    )
+    other = exchanged(update, 2 * members, 2)
+    (three,) = next_eliminated(
+        with_place(map_top, second_node, 0), front_entries3, update, other, SEP3 // BLK, False
+    )
     leaf_blocks = map_leaf[leaf_index]
-    spread = extend(update, leaf_blocks, order_one // BLK)
-    share_width = front_entries1.shape[1]
-    column_share = lax.dynamic_slice_in_dim(spread, column * share_width, share_width, 1)
-    entry_rows = front_entries1.shape[0]
-    offset = leaf_index % members * entry_rows
-    with_entries = lax.dynamic_slice_in_dim(column_share, offset, entry_rows, 0) + front_entries1
-    column_share = lax.dynamic_update_slice_in_dim(column_share, with_entries, offset, 0)
-    for bit_number in range(low_bits):
-        halfway = column_share.shape[0] // 2
-        upper_side = leaf_index >> bit_number & 1 == 1
-        kept_rows = jnp.where(upper_side, column_share[halfway:], column_share[:halfway])
-        sent_rows = jnp.where(upper_side, column_share[:halfway], column_share[halfway:])
-        column_share = kept_rows + partner_2(sent_rows, "leaf", bit_number)
-    for bit_number in reversed(range(low_bits)):
-        upper_side = leaf_index >> bit_number & 1 == 1
-        partner_rows = partner_2(column_share, "leaf", bit_number)
-        column_share = jnp.where(
-            upper_side,
-            jnp.concatenate([partner_rows, column_share], axis=0),
-            jnp.concatenate([column_share, partner_rows], axis=0),
-        )
-    front_one = lax.all_gather(column_share, "front", axis=1, tiled=True)
-    one = eliminated(front_one, SEP1 // BLK)
-    entries_two = lax.dynamic_slice_in_dim(front_entries2, second_node * order_two, order_two, 0)
-    two = ascended(one[SEP1:, SEP1:], low_bits, entries_two, map_mid, first_node, SEP2 // BLK)
-    three = ascended(
-        two[SEP2:, SEP2:], low_bits + 1, front_entries3, map_top, second_node, SEP3 // BLK
-    )
     own = jnp.broadcast_to(leaf_blocks[column], (4,))
     maps = jnp.stack([map_top[second_node], map_mid[first_node], leaf_blocks, own], axis=0)
     return back_substituted(maps, one, two, three)

time: 439 us -> 290 us (0.66); the launches traced: 434 us -> 290 us
  waiting for transfers between devices: 146 us -> 0 us
  Pallas kernels: 195 us -> 275 us
  starting transfers between devices: 42.7 us -> 0 us
  local copies, waits for them, and re-layouts: 29.8 us -> 12.3 us
  between operations: 13.8 us -> 0.1 us
    pallas_call x3 -> x6, Pallas kernels: 183 us -> 263 us  [the longest x2 138 us: next_eliminated(): pl.pallas_call(functools.partial(next_kernel, blocks, packs), out_shape=t...]
    all_gather x1 -> x0, waiting for transfers between devices: 52 us -> none  [body(): front_one = lax.all_gather(column_share, 'front', axis=1, tiled=True)]
    all_to_all x3 -> x0, waiting for transfers between devices: 50.9 us -> none  [sent_to_all(): return lax.all_to_all(copies, axis, split_axis=0, concat_axis=0, tiled=True)]
    ppermute x10 -> x0, waiting for transfers between devices: 43 us -> none  [partner_2(): return lax.ppermute(block, axis, route)]
    ppermute x10 -> x0, starting transfers between devices: 30.5 us -> none  [partner_2(): return lax.ppermute(block, axis, route)]
    all_to_all x3 -> x0, starting transfers between devices: 12.2 us -> none  [sent_to_all(): return lax.all_to_all(copies, axis, split_axis=0, concat_axis=0, tiled=True)]
    gather x3 -> x0, local copies, waits for them, and re-layouts: 9.34 us -> none  [the longest x2 7.32 us: extend(): picked = jnp.take(picked_rows, source, axis=2)]
    unnamed x7 -> x15, local copies, waits for them, and re-layouts: 0.11 us -> 7.18 us
  transfers between devices with their start and end apart: 14 -> 0, of which waited for: 14 -> 0; matrix products, arithmetic and copies ran while one was open for 2% -> 0% of each run, Pallas kernels for 0% -> 0%
where the time goes in v2:
time: 290 us
  Pallas kernels  275 us (95%)
  local copies, waits for them, and re-layouts  12.3 us (4%)
    pallas_call x2, Pallas kernels, next_eliminated(): pl.pallas_call(functools.partial(next_kernel, blocks, packs), out_shape=t...  138 us
    pallas_call x1, Pallas kernels, first_eliminated(): pl.pallas_call(functools.partial(first_kernel, blocks), out_shape=(jax.Sh...  46.4 us
    pallas_call x1, Pallas kernels, gathered(): pl.pallas_call(gather_kernel, out_shape=jax.ShapeDtypeStruct((36, BLK, BL...  43.6 us
    pallas_call x2, Pallas kernels, exchanged(): pl.pallas_call(functools.partial(exchange_kernel, distance), out_shape=ja...  35.1 us
    pallas_call x1, Pallas kernels, back_substituted(): pl.pallas_call(back_kernel, out_shape=jax.ShapeDtypeStruct((half, BLK), F...  12.1 us
    unnamed x15, local copies, waits for them, and re-layouts  7.18 us

profile of v2, /device:TPU:1, one launch (start us, length us, event | category | flops | bytes accessed | tf_op | source)
XLA Modules:
  0.0 290.2 jit_solution(3481314990202799657)
XLA Ops:
  0.0 1.3 dynamic_slice.30
  1.3 0.7 pad.9.clone
  2.0 0.8 constant_dynamic-slice_fusion
  2.8 0.1 pad.5.clone
  2.8 0.1 pad.2.clone
  2.9 0.6 add_add_fusion.2.map_ref
  3.6 0.6 add_add_fusion.1.map_ref
  4.2 0.8 constant_dynamic-slice_fusion.3
  5.0 0.1 copy.11
  5.1 0.6 add_add_fusion.map_ref
  5.7 0.8 constant_dynamic-slice_fusion.2
  6.4 0.8 slice_bitcast_fusion.3
  7.2 0.7 select_add_fusion.table_ref
  7.9 0.0 copy-start.5
  8.0 0.9 copy-done.5
  8.9 0.8 copy-done.6
  9.7 43.6 %shard_map.91.lower_ref = f32[36,128,128]{2,1,0:T(8,128)S(1)} custom-call(s32[36,16]{1,0:T(8,128)S(1)} %select_add_fusion.table_ref, f32[4,16,8,128]{3,2,1,0:T(8,128)S(1)} %bitcast.16, f32[64,256]{1,0:T(8,128)S(1)} %copy-done.6), custom_call_target="tpu_custom_call" | custom-call | tf_op jit(solution)/shard_map/pallas_call | solution.py:470
  53.4 0.0 copy-start
  53.4 1.4 copy-done
  54.8 46.4 %shard_map.92 = (f32[1024,1024]{1,0:T(8,128)}, f32[1280,128]{1,0:T(8,128)}) custom-call(f32[36,128,128]{2,1,0:T(8,128)} %copy-done), custom_call_target="tpu_custom_call" | custom-call | tf_op jit(solution)/shard_map/pallas_call | solution.py:505
  101.2 1.1 copy-done.1
  102.3 16.8 %shard_map.93.other_ref = f32[1280,128]{1,0:T(8,128)S(1)} custom-call(f32[1280,128]{1,0:T(8,128)S(1)} %copy-done.1), custom_call_target="tpu_custom_call" | custom-call | tf_op jit(solution)/shard_map/pallas_call | solution.py:491
  119.1 0.0 copy-start.3
  119.1 0.9 copy-done.3
  120.0 48.1 %shard_map.94 = (f32[1024,1024]{1,0:T(8,128)}, f32[1280,128]{1,0:T(8,128)}) custom-call(s32[3,4]{1,0:T(4,128)} %add_add_fusion.1.map_ref, f32[2048,1024]{1,0:T(8,128)} %entries_ref.4, f32[1280,128]{1,0:T(8,128)} %get-tuple-element.10.tri_ref.mine_ref, f32[1280,128]{1,0:T(8,128)} %copy-done.3), custom_call_target="tpu_custom_call" | custom-call | tf_op jit(solution)/shard_map/pallas_call | solution.py:523
  168.1 0.0 copy-start.2
  168.1 1.1 copy-done.2
  169.2 18.2 %shard_map.95.other_ref = f32[1280,128]{1,0:T(8,128)S(1)} custom-call(f32[1280,128]{1,0:T(8,128)S(1)} %copy-done.2), custom_call_target="tpu_custom_call" | custom-call | tf_op jit(solution)/shard_map/pallas_call | solution.py:491
  187.4 0.0 copy-start.4
  187.5 0.8 copy-done.4
  188.3 89.8 %shard_map.96.three_ref = f32[1024,1024]{1,0:T(8,128)} custom-call(s32[3,4]{1,0:T(4,128)} %add_add_fusion.2.map_ref, f32[1024,1024]{1,0:T(8,128)} %entries_ref.5, f32[1280,128]{1,0:T(8,128)} %get-tuple-element.12.tri_ref.mine_ref, f32[1280,128]{1,0:T(8,128)} %copy-done.4), custom_call_target="tpu_custom_call" | custom-call | tf_op jit(solution)/shard_map/pallas_call | solution.py:523
  278.1 12.1 %shard_map.97 = f32[512,128]{1,0:T(8,128)} custom-call(s32[4,4]{1,0:T(4,128)} %add_add_fusion.map_ref, f32[1024,1024]{1,0:T(8,128)} %get-tuple-element.9.one_ref, f32[1024,1024]{1,0:T(8,128)} %get-tuple-element.11.two_ref, f32[1024,1024]{1,0:T(8,128)} %shard_map.96.three_ref), custom_call_target="tpu_custom_call" | custom-call | tf_op jit(solution)/shard_map/pallas_call | solution.py:586
  (3 shorter events, 0.0 us)
Async XLA Ops:
  7.9 1.0 copy-start.5
  8.9 0.8 copy-start.6
  53.4 1.4 copy-start
  101.2 1.1 copy-start.1
  119.1 0.9 copy-start.3
  168.1 1.1 copy-start.2
  187.4 0.9 copy-start.4

commit v3 on v2

--- a/solution.py
+++ b/solution.py
@@ -21,17 +21,58 @@
     return jnp.broadcast_to(x[k : k + 1, :], (8, 128))
 
 
-def pick_row(x, k):
-    return jnp.take_along_axis(x, jnp.full((8, 128), k, jnp.int32), axis=0)
-
-
-def along(x, lanes):
-    return jnp.take_along_axis(x, lanes, axis=1)
+def along(x, c):
+    return jnp.take_along_axis(x, jnp.full((8, 128), c, jnp.int32), axis=1)
+
+
+def thirds(x):
+    high = x.astype(BF16)
+    rest = x - high.astype(F32)
+    middle = rest.astype(BF16)
+    return high, middle, (rest - middle.astype(F32)).astype(BF16)
+
+
+def outer(p, s):
+    ph, pm, pl_ = thirds(p)
+    sh, sm, sl = thirds(s)
+    left = jnp.concatenate([ph, ph, ph, pm, pm, pl_], axis=0)
+    right = jnp.concatenate([sh, sm, sl, sh, sm, sh], axis=0)
+    return lax.dot_general(left, right, (((0,), (0,)), ((), ())), preferred_element_type=F32)
+
+
+def swept_rows(rows, base, lane, sub):
+    e = [along(rows, base + j) for j in range(8)]
+    inside = (lane >= base) & (lane < base + 8)
+    m = jnp.where(lane == base + sub, -1.0, jnp.where(inside, 0.0, rows))
+    for k in range(0, 8, 2):
+        a, b, d = row_of(e[k], k), row_of(e[k + 1], k), row_of(e[k + 1], k + 1)
+        scale = 1.0 / (a * d - b * b)
+        first, cross, second = d * scale, b * scale, a * scale
+
+        def go(t):
+            upper, lower = row_of(t, k), row_of(t, k + 1)
+            new_upper = first * upper - cross * lower
+            new_lower = second * lower - cross * upper
+            y = t - (e[k] * new_upper + e[k + 1] * new_lower)
+            return jnp.where(sub == k, new_upper, jnp.where(sub == k + 1, new_lower, y))
+
+        m = go(m)
+        e = [go(x) if j > k + 1 else x for j, x in enumerate(e)]
+    return m
+
+
+def less_pivots(x, base, rows, inside):
+    total = None
+    for k in range(0, 8, 2):
+        term = along(x, base + k) * rows[k] + along(x, base + k + 1) * rows[k + 1]
+        total = term if total is None else total + term
+    return jnp.where(inside, 0.0, x) - total
 
 
 def invert(w):
     lane = lax.broadcasted_iota(jnp.int32, (8, 128), 1)
     sub = lax.broadcasted_iota(jnp.int32, (8, 128), 0)
+    lanes = lax.broadcasted_iota(jnp.int32, (128, 128), 1)
     tiles = [w[8 * i : 8 * i + 8, :] for i in range(16)]
     diagonal = [jnp.where(lane == 8 * i + sub, x, 0.0) for i, x in enumerate(tiles)]
     total = functools.reduce(jnp.add, diagonal)
@@ -42,34 +83,38 @@
     for i in range(16):
         w[8 * i : 8 * i + 8, :] = tiles[i] * down[i] * across
 
+    def at(t):
+        return pl.ds(pl.multiple_of(8 * t, 8), 8)
+
     def panel(p, carry):
+        rows, before, rows_before = carry
         base = 8 * p
-        here = pl.ds(pl.multiple_of(base, 8), 8)
-        tiles = [w[8 * i : 8 * i + 8, :] for i in range(16)]
-        pivot = w[here, :]
-        for k in range(0, 8, 2):
-            c = jnp.full((8, 128), base + k, jnp.int32)
-            at_first, at_second = lane == c, lane == c + 1
-            hit = at_first | at_second
-            first, second = along(pivot, c), along(pivot, c + 1)
-            a, b, d = pick_row(first, k), pick_row(first, k + 1), pick_row(second, k + 1)
-            upper = jnp.where(at_first, -1.0, jnp.where(at_second, 0.0, row_of(pivot, k)))
-            lower = jnp.where(at_second, -1.0, jnp.where(at_first, 0.0, row_of(pivot, k + 1)))
-            scale = 1.0 / (a * d - b * b)
-            new_first = (d * upper - b * lower) * scale
-            new_second = (a * lower - b * upper) * scale
-            tiles = [
-                jnp.where(hit, 0.0, x) - along(x, c) * new_first - along(x, c + 1) * new_second
-                for x in tiles
-            ]
-            pivot = jnp.where(hit, 0.0, pivot) - first * new_first - second * new_second
-            pivot = jnp.where(sub == k, new_first, jnp.where(sub == k + 1, new_second, pivot))
-        for i in range(16):
-            w[8 * i : 8 * i + 8, :] = tiles[i]
-        w[here, :] = pivot
-        return carry
-
-    lax.fori_loop(0, 16, panel, 0)
+        base_before = (base + 120) % 128
+        inside_before = (lane >= base - 8) & (lane < base)
+        following = w[at((p + 1) % 16), :]
+        now = swept_rows(rows, base, lane, sub)
+        following = less_pivots(
+            following, base_before, [row_of(before, k) for k in range(8)], inside_before
+        )
+        following = less_pivots(
+            following,
+            base,
+            [row_of(now, k) for k in range(8)],
+            (lane >= base) & (lane < base + 8),
+        )
+        gone = (lanes >= base - 8) & (lanes < base)
+        w[...] = jnp.where(gone, 0.0, w[...]) - outer(rows_before, before)
+
+        @pl.when(p > 0)
+        def _():
+            w[at(p - 1), :] = before
+
+        return following, now, rows
+
+    zero = jnp.zeros((8, 128), F32)
+    _, last, rows = lax.fori_loop(0, 16, panel, (w[0:8, :], zero, zero))
+    w[...] = jnp.where(lanes >= 120, 0.0, w[...]) - outer(rows, last)
+    w[120:128, :] = last
     for i in range(16):
         w[8 * i : 8 * i + 8, :] = -w[8 * i : 8 * i + 8, :] * down[i] * across
 
@@ -103,38 +148,34 @@
     return jnp.dot(a, b, preferred_element_type=F32)
 
 
-def eliminate(o, blocks, left, right, small_left, small_right, inverted, new_rows, new_columns):
+def eliminate(o, blocks, left, right, small_right, inverted):
     n = o.shape[0]
     whole = slice(None)
+    eye = (
+        lax.broadcasted_iota(jnp.int32, (BLK, BLK), 0)
+        == lax.broadcasted_iota(jnp.int32, (BLK, BLK), 1)
+    )
 
     def step(j, carry):
         at = pl.ds(pl.multiple_of(j * BLK, BLK), BLK)
         inverted[...] = o[at, at]
+        put_right(right, whole, o[at, :])
+        put_right(right, at, jnp.where(eye, -1.0, 0.0))
+        put_left(left, whole, o[:, at])
         invert(inverted)
-        block = inverted[...]
-        put_left(small_left, whole, block)
-        put_right(small_right, whole, block)
-        put_right(right, whole, o[at, :])
-        put_left(left, whole, o[:, at])
-        new_rows[...] = dot(small_left[...], right[...])
-
-        def column_tile(t, carry):
-            these = pl.ds(pl.multiple_of(t * 256, 256), 256)
-            new_columns[these, :] = dot(left[these, :], small_right[...])
-            return carry
-
-        lax.fori_loop(0, n // 256, column_tile, 0)
-        put_right(right, whole, new_rows[...])
+        put_right(small_right, whole, inverted[...])
+        for t in range(0, n, 256):
+            put_left(left, slice(t, t + 256), dot(left[t : t + 256, :], small_right[...]))
+        put_left(left, at, -inverted[...])
+        o[at, :] = jnp.zeros((BLK, n), F32)
+        o[:, at] = jnp.zeros((n, BLK), F32)
 
         def tile(t, carry):
-            these = pl.ds(pl.multiple_of(t * 256, 256), 256)
+            these = pl.ds(pl.multiple_of(t * 512, 512), 512)
             o[these, :] = o[these, :] - dot(left[these, :], right[...])
             return carry
 
-        lax.fori_loop(0, n // 256, tile, 0)
-        o[:, at] = new_columns[...]
-        o[at, :] = new_rows[...]
-        o[at, at] = -inverted[...]
+        lax.fori_loop(0, n // 512, tile, 0)
         return carry
 
     lax.fori_loop(0, blocks, step, 0)
@@ -144,11 +185,8 @@
     return [
         pltpu.VMEM((n, 4 * BLK), BF16),
         pltpu.VMEM((4 * BLK, n), BF16),
-        pltpu.VMEM((BLK, 4 * BLK), BF16),
         pltpu.VMEM((4 * BLK, BLK), BF16),
         pltpu.VMEM((BLK, BLK), F32),
-        pltpu.VMEM((BLK, n), F32),
-        pltpu.VMEM((n, BLK), F32),
     ]
 
 

time: 290 us -> 223 us (0.77)
  Pallas kernels: 275 us -> 207 us
    pallas_call x2, Pallas kernels: 138 us -> 87.9 us  [next_eliminated(): pl.pallas_call(functools.partial(next_kernel, blocks, packs), out_shape=t...]
    pallas_call x1, Pallas kernels: 46.4 us -> 29.7 us  [first_eliminated(): pl.pallas_call(functools.partial(first_kernel, blocks), out_shape=(jax.Sh...]
where the time goes in v3:
time: 223 us; the launch traced here: 222 us
  Pallas kernels  207 us (93%)
  local copies, waits for them, and re-layouts  12.3 us (6%)
  other arithmetic  2.67 us (1%)
    pallas_call x2, Pallas kernels, next_eliminated(): pl.pallas_call(functools.partial(next_kernel, blocks, packs), out_shape=t...  87.9 us
    pallas_call x1, Pallas kernels, gathered(): pl.pallas_call(gather_kernel, out_shape=jax.ShapeDtypeStruct((36, BLK, BL...  43.6 us
    pallas_call x2, Pallas kernels, exchanged(): pl.pallas_call(functools.partial(exchange_kernel, distance), out_shape=ja...  35.1 us
    pallas_call x1, Pallas kernels, first_eliminated(): pl.pallas_call(functools.partial(first_kernel, blocks), out_shape=(jax.Sh...  29.7 us
    pallas_call x1, Pallas kernels, back_substituted(): pl.pallas_call(back_kernel, out_shape=jax.ShapeDtypeStruct((half, BLK), F...  11 us
    unnamed x15, local copies, waits for them, and re-layouts  7.18 us

profile of v3, /device:TPU:1, one launch (start us, length us, event | category | flops | bytes accessed | tf_op | source)
XLA Modules:
  0.0 222.4 jit_solution(10121163176575975817)
XLA Ops:
  0.0 1.3 dynamic_slice.30
  1.3 0.7 pad.9.clone
  2.0 0.8 constant_dynamic-slice_fusion
  2.8 0.1 pad.5.clone
  2.8 0.1 pad.2.clone
  2.9 0.6 add_add_fusion.2.map_ref
  3.6 0.6 add_add_fusion.1.map_ref
  4.2 0.8 constant_dynamic-slice_fusion.3
  5.0 0.1 copy.11
  5.1 0.6 add_add_fusion.map_ref
  5.7 0.8 constant_dynamic-slice_fusion.2
  6.4 0.8 slice_bitcast_fusion.3
  7.2 0.7 select_add_fusion.table_ref
  7.9 0.0 copy-start.5
  8.0 0.9 copy-done.5
  8.9 0.8 copy-done.6
  9.7 43.6 %shard_map.91.lower_ref = f32[36,128,128]{2,1,0:T(8,128)S(1)} custom-call(s32[36,16]{1,0:T(8,128)S(1)} %select_add_fusion.table_ref, f32[4,16,8,128]{3,2,1,0:T(8,128)S(1)} %bitcast.16, f32[64,256]{1,0:T(8,128)S(1)} %copy-done.6), custom_call_target="tpu_custom_call" | custom-call | tf_op jit(solution)/shard_map/pallas_call | solution.py:508
  53.4 0.0 copy-start
  53.4 1.4 copy-done
  54.8 29.7 %shard_map.92 = (f32[1024,1024]{1,0:T(8,128)}, f32[1280,128]{1,0:T(8,128)}) custom-call(f32[36,128,128]{2,1,0:T(8,128)} %copy-done), custom_call_target="tpu_custom_call" | custom-call | tf_op jit(solution)/shard_map/pallas_call | solution.py:543
  84.5 1.1 copy-done.1
  85.6 16.6 %shard_map.93.other_ref = f32[1280,128]{1,0:T(8,128)S(1)} custom-call(f32[1280,128]{1,0:T(8,128)S(1)} %copy-done.1), custom_call_target="tpu_custom_call" | custom-call | tf_op jit(solution)/shard_map/pallas_call | solution.py:529
  102.2 0.0 copy-start.3
  102.2 0.9 copy-done.3
  103.1 31.4 %shard_map.94 = (f32[1024,1024]{1,0:T(8,128)}, f32[1280,128]{1,0:T(8,128)}) custom-call(s32[3,4]{1,0:T(4,128)} %add_add_fusion.1.map_ref, f32[2048,1024]{1,0:T(8,128)} %entries_ref.4, f32[1280,128]{1,0:T(8,128)} %get-tuple-element.10.tri_ref.mine_ref, f32[1280,128]{1,0:T(8,128)} %copy-done.3), custom_call_target="tpu_custom_call" | custom-call | tf_op jit(solution)/shard_map/pallas_call | solution.py:561
  134.6 0.0 copy-start.2
  134.6 1.1 copy-done.2
  135.6 18.5 %shard_map.95.other_ref = f32[1280,128]{1,0:T(8,128)S(1)} custom-call(f32[1280,128]{1,0:T(8,128)S(1)} %copy-done.2), custom_call_target="tpu_custom_call" | custom-call | tf_op jit(solution)/shard_map/pallas_call | solution.py:529
  154.1 0.0 copy-start.4
  154.1 0.8 copy-done.4
  155.0 56.4 %shard_map.96.three_ref = f32[1024,1024]{1,0:T(8,128)} custom-call(s32[3,4]{1,0:T(4,128)} %add_add_fusion.2.map_ref, f32[1024,1024]{1,0:T(8,128)} %entries_ref.5, f32[1280,128]{1,0:T(8,128)} %get-tuple-element.12.tri_ref.mine_ref, f32[1280,128]{1,0:T(8,128)} %copy-done.4), custom_call_target="tpu_custom_call" | custom-call | tf_op jit(solution)/shard_map/pallas_call | solution.py:561
  211.4 11.0 %shard_map.97 = f32[512,128]{1,0:T(8,128)} custom-call(s32[4,4]{1,0:T(4,128)} %add_add_fusion.map_ref, f32[1024,1024]{1,0:T(8,128)} %get-tuple-element.9.one_ref, f32[1024,1024]{1,0:T(8,128)} %get-tuple-element.11.two_ref, f32[1024,1024]{1,0:T(8,128)} %shard_map.96.three_ref), custom_call_target="tpu_custom_call" | custom-call | tf_op jit(solution)/shard_map/pallas_call | solution.py:624
  (3 shorter events, 0.0 us)
Async XLA Ops:
  7.9 1.0 copy-start.5
  8.9 0.8 copy-start.6
  53.4 1.4 copy-start
  84.5 1.1 copy-start.1
  102.2 0.9 copy-start.3
  134.6 1.1 copy-start.2
  154.1 0.9 copy-start.4

commit v4 on v3

--- a/solution.py
+++ b/solution.py
@@ -224,16 +224,11 @@
             o_ref[columns, rows] = o_ref[columns, rows] + part.T
 
 
-def next_kernel(blocks, packs, map_ref, entries_ref, mine_ref, other_ref, o_ref, *rest):
-    tri_ref, rest = (rest[0], rest[1:]) if packs else (None, rest)
-    copied, scratch = rest[0], rest[1:]
-    n = o_ref.shape[0]
-    start = pl.multiple_of(map_ref[2, 0] * n, 8)
-    fetch = pltpu.make_async_copy(entries_ref.at[pl.ds(start, n), :], o_ref, copied)
-    fetch.start()
-    fetch.wait()
-    add_child(o_ref, mine_ref, map_ref, 0)
-    add_child(o_ref, other_ref, map_ref, 1)
+def next_kernel(blocks, packs, members, map_ref, base_ref, mine_ref, other_ref, o_ref, *rest):
+    tri_ref, scratch = (rest[0], rest[1:]) if packs else (None, rest)
+    child = lax.axis_index("leaf") // members
+    add_child(o_ref, mine_ref, map_ref, child)
+    add_child(o_ref, other_ref, map_ref, child + 1 - 2 * (child % 2))
     eliminate(o_ref, blocks, *scratch)
     if packs:
         pack_update(o_ref, tri_ref)
@@ -259,8 +254,12 @@
     pl.semaphore_wait(barrier, len(devices))
 
 
-def exchange_kernel(distance, tri_ref, o_ref, sent, got):
+def exchange_kernel(distance, tri_ref, entries_ref, o_ref, base_ref, sent, got, copied):
     leaf, y = lax.axis_index("leaf"), lax.axis_index("front")
+    n = base_ref.shape[0]
+    start = pl.multiple_of((leaf // (2 * distance)) % (entries_ref.shape[0] // n) * n, 8)
+    fetch = pltpu.make_async_copy(entries_ref.at[pl.ds(start, n), :], base_ref, copied)
+    fetch.start()
     core, x = leaf % 2, (leaf // 2) % 4
     z = leaf // 8
     sibling = leaf + distance * (1 - 2 * ((leaf // distance) % 2))
@@ -313,11 +312,12 @@
         copy.wait_recv()
     for copy in [across] + spread + wide + last:
         copy.wait_send()
+    fetch.wait()
 
 
 def gather_kernel(
-    table_ref, leaf_ref, entries_ref, o_ref,
-    met, partial, halves_in, own_entries,
+    map_ref, leaf_ref, entries_ref, o_ref,
+    met, partial, halves_in, own_entries, found_tile, table, told,
     keep, sent, got, sent_e, got_e, sent_y, got_y, sent_x, got_x, sent_c, got_c,
 ):
     leaf, y = lax.axis_index("leaf"), lax.axis_index("front")
@@ -371,16 +371,34 @@
                 source, target, sent_e.at[g], got_e.at[high, y], base + to, target_y
             ).start()
 
+    lane = lax.broadcasted_iota(jnp.int32, (16, BLK), 1)
+    group = (
+        (lane >= 9).astype(jnp.int32) + (lane >= 18).astype(jnp.int32) + (lane >= 27).astype(jnp.int32)
+    )
+    within = lane - 9 * group
+    second = within > group
+    block_row = jnp.where(second, 7 - group, group)
+    block_column = jnp.where(second, within - group - 1, within)
+    maps = map_ref[pl.ds(pl.multiple_of(base, 16), 16), :]
+    found = jnp.full((16, BLK), 4, jnp.int32)
+    landing = jnp.zeros((16, BLK), jnp.int32)
+    for i in range(4):
+        target = jnp.broadcast_to(maps[:, i : i + 1], (16, BLK))
+        found = jnp.where(block_row == target, i, found)
+        landing = landing + target * jnp.where(y == i, 1, 0)
+    found_tile[...] = jnp.where(block_column == landing, found, 4)
+    tell = pltpu.make_async_copy(found_tile, table, told)
+    tell.start()
+    tell.wait()
     kept.wait()
     for copy in members:
         copy.wait_recv()
 
     def sum_block(t, carry):
-        total = met[table_ref[t, 0] // 5, table_ref[t, 0] % 5]
-        for s in range(1, 16):
-            index = table_ref[t, s]
-            total = total + met[index // 5, index % 5]
-        partial[t] = total
+        terms = [met[s, table[s, t]] for s in range(16)]
+        while len(terms) > 1:
+            terms = [terms[i] + terms[i + 1] for i in range(0, len(terms), 2)]
+        partial[t] = terms[0]
         return carry
 
     lax.fori_loop(0, 36, sum_block, 0)
@@ -500,42 +518,46 @@
 
 VMEM_SPEC = pl.BlockSpec(memory_space=pltpu.VMEM)
 SMEM_SPEC = pl.BlockSpec(memory_space=pltpu.SMEM)
-PARAMS = pltpu.CompilerParams(vmem_limit_bytes=60 * 1024 * 1024)
-
-
-def gathered(table, leaf_update, entries):
+PARAMS = pltpu.CompilerParams(vmem_limit_bytes=24 * 1024 * 1024)
+
+
+def gathered(map_leaf, leaf_update, entries):
     dma = pltpu.SemaphoreType.DMA
     return pl.pallas_call(
         gather_kernel,
         out_shape=jax.ShapeDtypeStruct((36, BLK, BLK), F32),
-        in_specs=[SMEM_SPEC, VMEM_SPEC, VMEM_SPEC],
+        in_specs=[VMEM_SPEC, VMEM_SPEC, VMEM_SPEC],
         out_specs=VMEM_SPEC,
         scratch_shapes=[
             pltpu.VMEM((16, 5, 8, BLK), F32),
             pltpu.VMEM((36, 8, BLK), F32),
             pltpu.VMEM((3, 9, 8, BLK), F32),
             pltpu.VMEM((2, 8, 1024), F32),
+            pltpu.VMEM((16, BLK), jnp.int32),
+            pltpu.SMEM((16, BLK), jnp.int32),
+            dma,
             dma((1,)), dma((16,)), dma((16,)), dma((8,)), dma((2, 4)), dma((8,)), dma((8,)),
             dma((12,)), dma((12,)), dma((16,)), dma((16,)),
         ],
         compiler_params=pltpu.CompilerParams(
             vmem_limit_bytes=32 * 1024 * 1024, collective_id=0, has_side_effects=True
         ),
-    )(table, leaf_update.reshape(4, 16, 8, BLK), entries)
-
-
-def exchanged(tri, distance, collective_id):
+    )(map_leaf, leaf_update.reshape(4, 16, 8, BLK), entries)
+
+
+def exchanged(tri, entries, distance, collective_id):
     dma = pltpu.SemaphoreType.DMA
+    n = 8 * BLK
     return pl.pallas_call(
         functools.partial(exchange_kernel, distance),
-        out_shape=jax.ShapeDtypeStruct(tri.shape, F32),
-        in_specs=[VMEM_SPEC],
-        out_specs=VMEM_SPEC,
-        scratch_shapes=[dma((11,)), dma((11,))],
+        out_shape=(jax.ShapeDtypeStruct(tri.shape, F32), jax.ShapeDtypeStruct((n, n), F32)),
+        in_specs=[VMEM_SPEC, pl.BlockSpec(memory_space=pltpu.HBM)],
+        out_specs=(VMEM_SPEC, VMEM_SPEC),
+        scratch_shapes=[dma((11,)), dma((11,)), dma],
         compiler_params=pltpu.CompilerParams(
-            vmem_limit_bytes=16 * 1024 * 1024, collective_id=collective_id, has_side_effects=True
+            vmem_limit_bytes=(43 if collective_id == 1 else 16) * 1024 * 1024, collective_id=collective_id, has_side_effects=True
         ),
-    )(tri)
+    )(tri, entries)
 
 
 def first_eliminated(lower, blocks):
@@ -553,19 +575,20 @@
     )(lower)
 
 
-def next_eliminated(maps, entries, mine, other, blocks, packs):
+def next_eliminated(maps, base, mine, other, blocks, packs, members):
     n = 8 * BLK
     out = [jax.ShapeDtypeStruct((n, n), F32)]
     if packs:
         out.append(jax.ShapeDtypeStruct((10 * BLK, BLK), F32))
     return pl.pallas_call(
-        functools.partial(next_kernel, blocks, packs),
+        functools.partial(next_kernel, blocks, packs, members),
         out_shape=tuple(out),
-        in_specs=[SMEM_SPEC, pl.BlockSpec(memory_space=pl.ANY), VMEM_SPEC, VMEM_SPEC],
+        in_specs=[SMEM_SPEC, VMEM_SPEC, VMEM_SPEC, VMEM_SPEC],
         out_specs=tuple([VMEM_SPEC] * len(out)),
-        scratch_shapes=[pltpu.SemaphoreType.DMA] + scratch_for(n),
+        scratch_shapes=scratch_for(n),
+        input_output_aliases={1: 0},
         compiler_params=PARAMS,
-    )(maps, entries, mine, other)
+    )(maps, base, mine, other)
 
 
 def column_of_inverse(swept, sigma, sigma_left, coupling_left, block, value, value_right, column):
@@ -590,41 +613,46 @@
 
 
 def back_kernel(
-    map_ref, one_ref, two_ref, three_ref, o_ref, sigma, sigma_left, coupling_left, value, value_right, column, lower
+    top_ref, mid_ref, leaf_ref, one_ref, two_ref, three_ref, o_ref, sigma, sigma_left, coupling_left, value, value_right, column, lower
 ):
     half = 4 * BLK
     whole = slice(None)
+    leaf = lax.axis_index("leaf")
+    first_node, second_node = leaf // 16, leaf // 32
     for i in range(4):
         for j in range(4):
-            picked = three_ref[at_block(map_ref[0, i]), at_block(map_ref[0, j])]
+            picked = three_ref[
+                at_block(top_ref[second_node, i]), at_block(top_ref[second_node, j])
+            ]
             sigma[i * BLK : (i + 1) * BLK, j * BLK : (j + 1) * BLK] = -picked
     put_left(sigma_left, whole, sigma[...])
     put_left(coupling_left, whole, two_ref[:half, half:])
 
     def step(j, carry):
         column_of_inverse(
-            two_ref, sigma, sigma_left, coupling_left, map_ref[1, j], value, value_right, column
+            two_ref, sigma, sigma_left, coupling_left, mid_ref[first_node, j], value, value_right, column
         )
         for i in range(4):
-            lower[i * BLK : (i + 1) * BLK, at_block(j)] = column[at_block(map_ref[1, i]), :]
+            lower[i * BLK : (i + 1) * BLK, at_block(j)] = column[at_block(mid_ref[first_node, i]), :]
         return carry
 
     lax.fori_loop(0, 4, step, 0)
     put_left(sigma_left, whole, lower[...])
     put_left(coupling_left, whole, one_ref[:half, half:])
     column_of_inverse(
-        one_ref, lower, sigma_left, coupling_left, map_ref[3, 0], value, value_right, column
+        one_ref, lower, sigma_left, coupling_left, leaf_ref[leaf, lax.axis_index("front")],
+        value, value_right, column,
     )
     for i in range(4):
-        o_ref[i * BLK : (i + 1) * BLK, :] = column[at_block(map_ref[2, i]), :]
-
-
-def back_substituted(maps, one, two, three):
+        o_ref[i * BLK : (i + 1) * BLK, :] = column[at_block(leaf_ref[leaf, i]), :]
+
+
+def back_substituted(top, mid, leaf, one, two, three):
     half = 4 * BLK
     return pl.pallas_call(
         back_kernel,
         out_shape=jax.ShapeDtypeStruct((half, BLK), F32),
-        in_specs=[SMEM_SPEC, VMEM_SPEC, VMEM_SPEC, VMEM_SPEC],
+        in_specs=[SMEM_SPEC] * 3 + [VMEM_SPEC] * 3,
         out_specs=VMEM_SPEC,
         scratch_shapes=[
             pltpu.VMEM((half, half), F32),
@@ -636,43 +664,18 @@
             pltpu.VMEM((half, half), F32),
         ],
         compiler_params=PARAMS,
-    )(maps, one, two, three)
-
-
-def with_place(maps, child, place):
-    sibling = child + 1 - 2 * (child % 2)
-    return jnp.stack([maps[child], maps[sibling], jnp.broadcast_to(place, (4,))], axis=0)
+    )(top, mid, leaf, one, two, three)
 
 
 def body(leaf_update, front_entries1, front_entries2, front_entries3, map_leaf, map_mid, map_top):
-    leaf_index = lax.axis_index("leaf")
-    column = lax.axis_index("front")
     members = lax.axis_size("leaf") // 4
-    first_node = leaf_index // members
-    second_node = leaf_index // (2 * members)
-    below = lax.dynamic_slice_in_dim(map_leaf, first_node * members, members, 0)
-    rows = jnp.array([a for a, _ in LOWER], jnp.int32)[:, None]
-    columns = jnp.array([b for _, b in LOWER], jnp.int32)[:, None]
-    found = jnp.full((len(LOWER), members), 4, jnp.int32)
-    for i in range(4):
-        found = jnp.where(rows == below[:, i][None, :], i, found)
-    landing = lax.dynamic_index_in_dim(below, column, 1, keepdims=False)
-    found = jnp.where(columns == landing[None, :], found, 4)
-    table = found + 5 * jnp.arange(members, dtype=jnp.int32)[None, :]
-    lower = gathered(table, leaf_update, front_entries1)
+    lower = gathered(map_leaf, leaf_update, front_entries1)
     one, update = first_eliminated(lower, SEP1 // BLK)
-    other = exchanged(update, members, 1)
-    two, update = next_eliminated(
-        with_place(map_mid, first_node, second_node), front_entries2, update, other, SEP2 // BLK, True
-    )
-    other = exchanged(update, 2 * members, 2)
-    (three,) = next_eliminated(
-        with_place(map_top, second_node, 0), front_entries3, update, other, SEP3 // BLK, False
-    )
-    leaf_blocks = map_leaf[leaf_index]
-    own = jnp.broadcast_to(leaf_blocks[column], (4,))
-    maps = jnp.stack([map_top[second_node], map_mid[first_node], leaf_blocks, own], axis=0)
-    return back_substituted(maps, one, two, three)
+    other, base = exchanged(update, front_entries2, members, 1)
+    two, update = next_eliminated(map_mid, base, update, other, SEP2 // BLK, True, members)
+    other, base = exchanged(update, front_entries3, 2 * members, 2)
+    (three,) = next_eliminated(map_top, base, update, other, SEP3 // BLK, False, 2 * members)
+    return back_substituted(map_top, map_mid, map_leaf, one, two, three)
 
 
 def solution(mesh):

time: 223 us -> 189 us (0.85)
  Pallas kernels: 207 us -> 185 us
  local copies, waits for them, and re-layouts: 12.3 us -> 2.58 us
  other arithmetic: 2.67 us -> 0 us
    pallas_call x4, Pallas kernels: 123 us -> 114 us  [the longest x2 78 us: next_eliminated(): pl.pallas_call(functools.partial(next_kernel, blocks, packs, members), ou...]
    pallas_call x1, Pallas kernels: 43.6 us -> 38.8 us  [gathered(): pl.pallas_call(gather_kernel, out_shape=jax.ShapeDtypeStruct((36, BLK, BL...]
    unnamed x15 -> x11, local copies, waits for them, and re-layouts: 7.18 us -> 2.58 us
    pallas_call x1, Pallas kernels: 11 us -> 6.88 us  [back_substituted(): pl.pallas_call(back_kernel, out_shape=jax.ShapeDtypeStruct((half, BLK), F...]
    pallas_call x1, Pallas kernels: 29.7 us -> 25.8 us  [first_eliminated(): pl.pallas_call(functools.partial(first_kernel, blocks), out_shape=(jax.Sh...]
    dynamic_slice x4 -> x0, local copies, waits for them, and re-layouts: 3.56 us -> none  [the longest x1 1.29 us: body(): own = jnp.broadcast_to(leaf_blocks[column], (4,))]
where the time goes in v4:
time: 189 us; the launch traced here: 188 us
  Pallas kernels  185 us (98%)
  local copies, waits for them, and re-layouts  2.58 us (1%)
    pallas_call x2, Pallas kernels, next_eliminated(): pl.pallas_call(functools.partial(next_kernel, blocks, packs, members), ou...  78 us
    pallas_call x1, Pallas kernels, gathered(): pl.pallas_call(gather_kernel, out_shape=jax.ShapeDtypeStruct((36, BLK, BL...  38.8 us
    pallas_call x2, Pallas kernels, exchanged(): pl.pallas_call(functools.partial(exchange_kernel, distance), out_shape=(j...  36 us
    pallas_call x1, Pallas kernels, first_eliminated(): pl.pallas_call(functools.partial(first_kernel, blocks), out_shape=(jax.Sh...  25.8 us
    pallas_call x1, Pallas kernels, back_substituted(): pl.pallas_call(back_kernel, out_shape=jax.ShapeDtypeStruct((half, BLK), F...  6.88 us

profile of v4, /device:TPU:1, one launch (start us, length us, event | category | flops | bytes accessed | tf_op | source)
XLA Modules:
  0.0 188.2 jit_solution(4596729821136324717)
XLA Ops:
  0.0 0.8 copy.11.map_ref.leaf_ref
  0.8 0.0 copy-start.1
  0.8 0.9 copy-done.1
  1.7 0.0 copy-start.2
  1.7 0.8 copy-done.2
  2.6 38.8 %shard_map.73.lower_ref = f32[36,128,128]{2,1,0:T(8,128)S(1)} custom-call(s32[64,4]{1,0:T(8,128)S(1)} %copy.11.map_ref.leaf_ref, f32[4,16,8,128]{3,2,1,0:T(8,128)S(1)} %bitcast.1, f32[64,256]{1,0:T(8,128)S(1)} %copy-done.2), custom_call_target="tpu_custom_call" | custom-call | tf_op jit(solution)/shard_map/pallas_call | solution.py:526
  41.3 25.8 %shard_map.74 = (f32[1024,1024]{1,0:T(8,128)S(1)}, f32[1280,128]{1,0:T(8,128)S(1)}) custom-call(f32[36,128,128]{2,1,0:T(8,128)S(1)} %shard_map.73.lower_ref), custom_call_target="tpu_custom_call" | custom-call | tf_op jit(solution)/shard_map/pallas_call | solution.py:565
  67.2 0.0 copy-start.3
  67.2 17.3 %shard_map.75 = (f32[1280,128]{1,0:T(8,128)S(1)}, f32[1024,1024]{1,0:T(8,128)S(1)}) custom-call(f32[1280,128]{1,0:T(8,128)S(1)} %get-tuple-element.14.tri_ref.mine_ref, f32[2048,1024]{1,0:T(8,128)} %entries_ref.4), custom_call_target="tpu_custom_call" | custom-call | tf_op jit(solution)/shard_map/pallas_call | solution.py:551
  84.5 0.0 copy-start
  84.5 0.0 copy-done.3
  84.5 0.0 copy-start.4
  84.5 26.4 %shard_map.76 = (f32[1024,1024]{1,0:T(8,128)S(1)}, f32[1280,128]{1,0:T(8,128)S(1)}) custom-call(s32[4,4]{1,0:T(4,128)S(1)} %copy-done.3, f32[1024,1024]{1,0:T(8,128)S(1)} %get-tuple-element.15.base_ref, f32[1280,128]{1,0:T(8,128)S(1)} %get-tuple-element.14.tri_ref.mine_ref, f32[1280,128]{1,0:T(8,128)S(1)} %get-tuple-element.16.other_ref), custom_call_target="tpu_custom_call", output_to_operand_aliasing={{0}: (1, {})} | custom-call | tf_op jit(solution)/shard_map/pallas_call | solution.py:583
  110.9 0.0 copy-done
  110.9 18.8 %shard_map.77 = (f32[1280,128]{1,0:T(8,128)S(1)}, f32[1024,1024]{1,0:T(8,128)S(1)}) custom-call(f32[1280,128]{1,0:T(8,128)S(1)} %get-tuple-element.18.tri_ref.mine_ref, f32[1024,1024]{1,0:T(8,128)S(1)} %copy-done), custom_call_target="tpu_custom_call" | custom-call | tf_op jit(solution)/shard_map/pallas_call | solution.py:551
  129.7 0.0 copy-done.4
  129.7 51.6 %shard_map.78.three_ref = f32[1024,1024]{1,0:T(8,128)S(1)} custom-call(s32[2,4]{1,0:T(2,128)S(1)} %copy-done.4, f32[1024,1024]{1,0:T(8,128)S(1)} %get-tuple-element.19.base_ref, f32[1280,128]{1,0:T(8,128)S(1)} %get-tuple-element.18.tri_ref.mine_ref, f32[1280,128]{1,0:T(8,128)S(1)} %get-tuple-element.20.other_ref), custom_call_target="tpu_custom_call", output_to_operand_aliasing={{}: (1, {})} | custom-call | tf_op jit(solution)/shard_map/pallas_call | solution.py:583
  181.3 6.9 %shard_map.79 = f32[512,128]{1,0:T(8,128)} custom-call(s32[2,4]{1,0:T(2,128)S(1)} %copy-done.4, s32[4,4]{1,0:T(4,128)S(1)} %copy-done.3, s32[64,4]{1,0:T(8,128)S(1)} %copy.11.map_ref.leaf_ref, f32[1024,1024]{1,0:T(8,128)S(1)} %get-tuple-element.13.one_ref, f32[1024,1024]{1,0:T(8,128)S(1)} %get-tuple-element.17.two_ref, f32[1024,1024]{1,0:T(8,128)S(1)} %shard_map.78.three_ref), custom_call_target="tpu_custom_call" | custom-call | tf_op jit(solution)/shard_map/pallas_call | solution.py:652
Async XLA Ops:
  0.8 0.9 copy-start.1
  1.7 0.8 copy-start.2
  67.2 17.3 %copy-start.3 = (s32[4,4]{1,0:T(4,128)S(1)}, s32[4,4]{1,0:T(4,128)}, u32[]{:S(2)}) copy-start(s32[4,4]{1,0:T(4,128)} %mid_ref.1) | copy-start | bytes 196
  84.5 26.4 %copy-start = (f32[1024,1024]{1,0:T(8,128)S(1)}, f32[1024,1024]{1,0:T(8,128)}, u32[]{:S(2)}) copy-start(f32[1024,1024]{1,0:T(8,128)} %entries_ref.5) | copy-start | bytes 12582916
  84.5 45.2 %copy-start.4 = (s32[2,4]{1,0:T(2,128)S(1)}, s32[2,4]{1,0:T(2,128)}, u32[]{:S(2)}) copy-start(s32[2,4]{1,0:T(2,128)} %top_ref.1) | copy-start | bytes 100

commit v5 on v4

--- a/solution.py
+++ b/solution.py
@@ -15,6 +15,7 @@
 
 
 F32, BF16 = jnp.float32, jnp.bfloat16
+ROUNDS = 4
 
 
 def row_of(x, k):
@@ -32,12 +33,14 @@
     return high, middle, (rest - middle.astype(F32)).astype(BF16)
 
 
-def outer(p, s):
-    ph, pm, pl_ = thirds(p)
-    sh, sm, sl = thirds(s)
-    left = jnp.concatenate([ph, ph, ph, pm, pm, pl_], axis=0)
-    right = jnp.concatenate([sh, sm, sl, sh, sm, sh], axis=0)
-    return lax.dot_general(left, right, (((0,), (0,)), ((), ())), preferred_element_type=F32)
+def outer_left(p):
+    high, middle, low = thirds(p)
+    return jnp.concatenate([high, high, high, middle, middle, low], axis=0).T
+
+
+def outer_right(s):
+    high, middle, low = thirds(s)
+    return jnp.concatenate([high, middle, low, high, middle, high], axis=0)
 
 
 def swept_rows(rows, base, lane, sub):
@@ -46,19 +49,26 @@
     m = jnp.where(lane == base + sub, -1.0, jnp.where(inside, 0.0, rows))
     for k in range(0, 8, 2):
         a, b, d = row_of(e[k], k), row_of(e[k + 1], k), row_of(e[k + 1], k + 1)
+        is_first, is_second = sub == k, sub == k + 1
+        pair = is_first | is_second
+        left = jnp.where(is_first, -1.0, jnp.where(is_second, 0.0, e[k]))
+        right = jnp.where(is_second, -1.0, jnp.where(is_first, 0.0, e[k + 1]))
         scale = 1.0 / (a * d - b * b)
-        first, cross, second = d * scale, b * scale, a * scale
+        by_first = (d * left - b * right) * scale
+        by_second = (a * right - b * left) * scale
 
         def go(t):
-            upper, lower = row_of(t, k), row_of(t, k + 1)
-            new_upper = first * upper - cross * lower
-            new_lower = second * lower - cross * upper
-            y = t - (e[k] * new_upper + e[k + 1] * new_lower)
-            return jnp.where(sub == k, new_upper, jnp.where(sub == k + 1, new_lower, y))
+            return jnp.where(pair, 0.0, t) - by_first * row_of(t, k) - by_second * row_of(t, k + 1)
 
         m = go(m)
         e = [go(x) if j > k + 1 else x for j, x in enumerate(e)]
     return m
+
+
+def sum_of(terms):
+    while len(terms) > 1:
+        terms = [terms[i] + terms[i + 1] for i in range(0, len(terms), 2)]
+    return terms[0]
 
 
 def less_pivots(x, base, rows, inside):
@@ -69,10 +79,9 @@
     return jnp.where(inside, 0.0, x) - total
 
 
-def invert(w):
+def scaled_diagonal(w):
     lane = lax.broadcasted_iota(jnp.int32, (8, 128), 1)
     sub = lax.broadcasted_iota(jnp.int32, (8, 128), 0)
-    lanes = lax.broadcasted_iota(jnp.int32, (128, 128), 1)
     tiles = [w[8 * i : 8 * i + 8, :] for i in range(16)]
     diagonal = [jnp.where(lane == 8 * i + sub, x, 0.0) for i, x in enumerate(tiles)]
     total = functools.reduce(jnp.add, diagonal)
@@ -82,38 +91,55 @@
     ]
     for i in range(16):
         w[8 * i : 8 * i + 8, :] = tiles[i] * down[i] * across
+    return down, across
+
+
+def invert(w, rounds, beside):
+    lane = lax.broadcasted_iota(jnp.int32, (8, 128), 1)
+    sub = lax.broadcasted_iota(jnp.int32, (8, 128), 0)
+    lanes = lax.broadcasted_iota(jnp.int32, (128, 128), 1)
+    down, across = scaled_diagonal(w)
 
     def at(t):
         return pl.ds(pl.multiple_of(8 * t, 8), 8)
 
     def panel(p, carry):
-        rows, before, rows_before = carry
+        rows, before, left_before = carry
         base = 8 * p
         base_before = (base + 120) % 128
         inside_before = (lane >= base - 8) & (lane < base)
-        following = w[at((p + 1) % 16), :]
+        gone = (lanes >= base - 8) & (lanes < base)
+        q = (p + 1) % 16
+        following = w[at(q), :]
         now = swept_rows(rows, base, lane, sub)
+        own = lane == 8 * q + sub
+        entries = [
+            jnp.broadcast_to(
+                jnp.sum(jnp.where(own, row_of(rows, k), 0.0), axis=1, keepdims=True), (8, 128)
+            )
+            for k in range(8)
+        ]
         following = less_pivots(
             following, base_before, [row_of(before, k) for k in range(8)], inside_before
         )
-        following = less_pivots(
-            following,
-            base,
-            [row_of(now, k) for k in range(8)],
-            (lane >= base) & (lane < base + 8),
-        )
-        gone = (lanes >= base - 8) & (lanes < base)
-        w[...] = jnp.where(gone, 0.0, w[...]) - outer(rows_before, before)
-
-        @pl.when(p > 0)
-        def _():
-            w[at(p - 1), :] = before
-
-        return following, now, rows
-
-    zero = jnp.zeros((8, 128), F32)
-    _, last, rows = lax.fori_loop(0, 16, panel, (w[0:8, :], zero, zero))
-    w[...] = jnp.where(lanes >= 120, 0.0, w[...]) - outer(rows, last)
+        inside = (lane >= base) & (lane < base + 8)
+        following = jnp.where(inside, 0.0, following) - sum_of(
+            [entries[k] * row_of(now, k) for k in range(8)]
+        )
+        w[:BLK, :] = jnp.where(gone, 0.0, w[:BLK, :]) - dot(left_before, outer_right(before))
+        w[at((p + 16) % 17), :] = before
+        return following, now, outer_left(rows)
+
+    def turn(r, carry):
+        for p in range(16 // rounds):
+            carry = panel(r * (16 // rounds) + p, carry)
+            if p == 0:
+                beside(r)
+        return carry
+
+    start = (w[0:8, :], jnp.zeros((8, 128), F32), jnp.zeros((BLK, 48), BF16))
+    _, last, left = lax.fori_loop(0, rounds, turn, start)
+    w[:BLK, :] = jnp.where(lanes >= 120, 0.0, w[:BLK, :]) - dot(left, outer_right(last))
     w[120:128, :] = last
     for i in range(16):
         w[8 * i : 8 * i + 8, :] = -w[8 * i : 8 * i + 8, :] * down[i] * across
@@ -156,29 +182,43 @@
         == lax.broadcasted_iota(jnp.int32, (BLK, BLK), 1)
     )
 
-    def step(j, carry):
+    def nothing(r):
+        pass
+
+    def prepare(j):
         at = pl.ds(pl.multiple_of(j * BLK, BLK), BLK)
-        inverted[...] = o[at, at]
         put_right(right, whole, o[at, :])
         put_right(right, at, jnp.where(eye, -1.0, 0.0))
         put_left(left, whole, o[:, at])
-        invert(inverted)
-        put_right(small_right, whole, inverted[...])
+        put_right(small_right, whole, inverted[:BLK, :])
         for t in range(0, n, 256):
             put_left(left, slice(t, t + 256), dot(left[t : t + 256, :], small_right[...]))
-        put_left(left, at, -inverted[...])
+        put_left(left, at, -inverted[:BLK, :])
         o[at, :] = jnp.zeros((BLK, n), F32)
         o[:, at] = jnp.zeros((n, BLK), F32)
 
-        def tile(t, carry):
-            these = pl.ds(pl.multiple_of(t * 512, 512), 512)
-            o[these, :] = o[these, :] - dot(left[these, :], right[...])
-            return carry
-
-        lax.fori_loop(0, n // 512, tile, 0)
+    def update(size, t):
+        these = pl.ds(pl.multiple_of(t * size, size), size)
+        o[these, :] = o[these, :] - dot(left[these, :], right[...])
+
+    inverted[:BLK, :] = o[:BLK, :BLK]
+    invert(inverted, 16, nothing)
+
+    def step(j, carry):
+        prepare(j)
+        after = pl.ds(pl.multiple_of((j + 1) * BLK, BLK), BLK)
+        inverted[:BLK, :] = o[after, after] - dot(left[after, :], right[:, after])
+        invert(inverted, ROUNDS, functools.partial(update, n // ROUNDS))
         return carry
 
-    lax.fori_loop(0, blocks, step, 0)
+    lax.fori_loop(0, blocks - 1, step, 0)
+    prepare(blocks - 1)
+
+    def tile(t, carry):
+        update(512, t)
+        return carry
+
+    lax.fori_loop(0, n // 512, tile, 0)
 
 
 def scratch_for(n):
@@ -186,7 +226,7 @@
         pltpu.VMEM((n, 4 * BLK), BF16),
         pltpu.VMEM((4 * BLK, n), BF16),
         pltpu.VMEM((4 * BLK, BLK), BF16),
-        pltpu.VMEM((BLK, BLK), F32),
+        pltpu.VMEM((BLK + 8, BLK), F32),
     ]
 
 

time: 189 us -> 160 us (0.85)
  Pallas kernels: 185 us -> 156 us
    pallas_call x2, Pallas kernels: 78 us -> 55.5 us  [next_eliminated(): pl.pallas_call(functools.partial(next_kernel, blocks, packs, members), ou...]
    pallas_call x1, Pallas kernels: 25.8 us -> 18.5 us  [first_eliminated(): pl.pallas_call(functools.partial(first_kernel, blocks), out_shape=(jax.Sh...]
where the time goes in v5:
time: 160 us; the launch traced here: 159 us
  Pallas kernels  156 us (98%)
  local copies, waits for them, and re-layouts  2.58 us (2%)
    pallas_call x2, Pallas kernels, next_eliminated(): pl.pallas_call(functools.partial(next_kernel, blocks, packs, members), ou...  55.5 us
    pallas_call x1, Pallas kernels, gathered(): pl.pallas_call(gather_kernel, out_shape=jax.ShapeDtypeStruct((36, BLK, BL...  38.8 us
    pallas_call x2, Pallas kernels, exchanged(): pl.pallas_call(functools.partial(exchange_kernel, distance), out_shape=(j...  36.1 us
    pallas_call x1, Pallas kernels, first_eliminated(): pl.pallas_call(functools.partial(first_kernel, blocks), out_shape=(jax.Sh...  18.5 us
    pallas_call x1, Pallas kernels, back_substituted(): pl.pallas_call(back_kernel, out_shape=jax.ShapeDtypeStruct((half, BLK), F...  7.48 us

profile of v5, /device:TPU:1, one launch (start us, length us, event | category | flops | bytes accessed | tf_op | source)
XLA Modules:
  0.0 159.1 jit_solution(16660763852338745602)
XLA Ops:
  0.0 0.8 copy.11.map_ref.leaf_ref
  0.8 0.0 copy-start.1
  0.8 0.9 copy-done.1
  1.7 0.0 copy-start.2
  1.7 0.8 copy-done.2
  2.6 38.8 %shard_map.73.lower_ref = f32[36,128,128]{2,1,0:T(8,128)S(1)} custom-call(s32[64,4]{1,0:T(8,128)S(1)} %copy.11.map_ref.leaf_ref, f32[4,16,8,128]{3,2,1,0:T(8,128)S(1)} %bitcast.1, f32[64,256]{1,0:T(8,128)S(1)} %copy-done.2), custom_call_target="tpu_custom_call" | custom-call | tf_op jit(solution)/shard_map/pallas_call | solution.py:566
  41.3 18.5 %shard_map.74 = (f32[1024,1024]{1,0:T(8,128)S(1)}, f32[1280,128]{1,0:T(8,128)S(1)}) custom-call(f32[36,128,128]{2,1,0:T(8,128)S(1)} %shard_map.73.lower_ref), custom_call_target="tpu_custom_call" | custom-call | tf_op jit(solution)/shard_map/pallas_call | solution.py:605
  59.9 0.0 copy-start.3
  59.9 17.3 %shard_map.75 = (f32[1280,128]{1,0:T(8,128)S(1)}, f32[1024,1024]{1,0:T(8,128)S(1)}) custom-call(f32[1280,128]{1,0:T(8,128)S(1)} %get-tuple-element.14.tri_ref.mine_ref, f32[2048,1024]{1,0:T(8,128)} %entries_ref.4), custom_call_target="tpu_custom_call" | custom-call | tf_op jit(solution)/shard_map/pallas_call | solution.py:591
  77.2 0.0 copy-start
  77.2 0.0 copy-done.3
  77.2 0.0 copy-start.4
  77.2 19.1 %shard_map.76 = (f32[1024,1024]{1,0:T(8,128)S(1)}, f32[1280,128]{1,0:T(8,128)S(1)}) custom-call(s32[4,4]{1,0:T(4,128)S(1)} %copy-done.3, f32[1024,1024]{1,0:T(8,128)S(1)} %get-tuple-element.15.base_ref, f32[1280,128]{1,0:T(8,128)S(1)} %get-tuple-element.14.tri_ref.mine_ref, f32[1280,128]{1,0:T(8,128)S(1)} %get-tuple-element.16.other_ref), custom_call_target="tpu_custom_call", output_to_operand_aliasing={{0}: (1, {})} | custom-call | tf_op jit(solution)/shard_map/pallas_call | solution.py:623
  96.4 0.0 copy-done
  96.4 18.8 %shard_map.77 = (f32[1280,128]{1,0:T(8,128)S(1)}, f32[1024,1024]{1,0:T(8,128)S(1)}) custom-call(f32[1280,128]{1,0:T(8,128)S(1)} %get-tuple-element.18.tri_ref.mine_ref, f32[1024,1024]{1,0:T(8,128)S(1)} %copy-done), custom_call_target="tpu_custom_call" | custom-call | tf_op jit(solution)/shard_map/pallas_call | solution.py:591
  115.2 0.0 copy-done.4
  115.2 36.4 %shard_map.78.three_ref = f32[1024,1024]{1,0:T(8,128)S(1)} custom-call(s32[2,4]{1,0:T(2,128)S(1)} %copy-done.4, f32[1024,1024]{1,0:T(8,128)S(1)} %get-tuple-element.19.base_ref, f32[1280,128]{1,0:T(8,128)S(1)} %get-tuple-element.18.tri_ref.mine_ref, f32[1280,128]{1,0:T(8,128)S(1)} %get-tuple-element.20.other_ref), custom_call_target="tpu_custom_call", output_to_operand_aliasing={{}: (1, {})} | custom-call | tf_op jit(solution)/shard_map/pallas_call | solution.py:623
  151.6 7.5 %shard_map.79 = f32[512,128]{1,0:T(8,128)} custom-call(s32[2,4]{1,0:T(2,128)S(1)} %copy-done.4, s32[4,4]{1,0:T(4,128)S(1)} %copy-done.3, s32[64,4]{1,0:T(8,128)S(1)} %copy.11.map_ref.leaf_ref, f32[1024,1024]{1,0:T(8,128)S(1)} %get-tuple-element.13.one_ref, f32[1024,1024]{1,0:T(8,128)S(1)} %get-tuple-element.17.two_ref, f32[1024,1024]{1,0:T(8,128)S(1)} %shard_map.78.three_ref), custom_call_target="tpu_custom_call" | custom-call | tf_op jit(solution)/shard_map/pallas_call | solution.py:692
Async XLA Ops:
  0.8 0.9 copy-start.1
  1.7 0.8 copy-start.2
  59.9 17.3 %copy-start.3 = (s32[4,4]{1,0:T(4,128)S(1)}, s32[4,4]{1,0:T(4,128)}, u32[]{:S(2)}) copy-start(s32[4,4]{1,0:T(4,128)} %mid_ref.1) | copy-start | bytes 196
  77.2 19.2 %copy-start = (f32[1024,1024]{1,0:T(8,128)S(1)}, f32[1024,1024]{1,0:T(8,128)}, u32[]{:S(2)}) copy-start(f32[1024,1024]{1,0:T(8,128)} %entries_ref.5) | copy-start | bytes 12582916
  77.2 38.0 %copy-start.4 = (s32[2,4]{1,0:T(2,128)S(1)}, s32[2,4]{1,0:T(2,128)}, u32[]{:S(2)}) copy-start(s32[2,4]{1,0:T(2,128)} %top_ref.1) | copy-start | bytes 100

commit v6 on v5

--- a/solution.py
+++ b/solution.py
@@ -305,52 +305,39 @@
     sibling = leaf + distance * (1 - 2 * ((leaf // distance) % 2))
     other_core = leaf + 1 - 2 * core
     rows = tri_ref.shape[0] // 32
-
-    def in_x(d):
-        return z * 8 + ((x + d) % 4) * 2 + core
-
-    greet(
-        [(sibling, y), (other_core, y)]
-        + [(leaf, (y + d) % 4) for d in (1, 2, 3)]
-        + [(in_x(d), y) for d in (1, 2, 3)]
-    )
+    apart = [(dx, dy) for dx in (0, 1, 3, 2) for dy in (0, 1, 3, 2)]
+
+    def place(dx, dy):
+        return z * 8 + ((x + dx) % 4) * 2 + core, (y + dy) % 4
+
+    greet([(sibling, y), (other_core, y)] + [place(dx, dy) for dx, dy in apart[1:]])
 
     def share(c, xx, yy):
         return pl.ds(pl.multiple_of(((c * 4 + xx) * 4 + yy) * rows, 8), rows)
-
-    def row(c, xx):
-        return pl.ds(pl.multiple_of((c * 4 + xx) * 4 * rows, 8), 4 * rows)
 
     mine = share(core, x, y)
     across = remote(tri_ref.at[mine], o_ref.at[mine], sent.at[0], got.at[0], sibling, y)
     across.start()
     across.wait_recv()
-    spread = [
-        remote(o_ref.at[mine], o_ref.at[mine], sent.at[d], got.at[d], leaf, (y + d) % 4)
-        for d in (1, 2, 3)
-    ]
-    for copy in spread:
-        copy.start()
-    for copy in spread:
-        copy.wait_recv()
-    whole = row(core, x)
-    wide = [
-        remote(o_ref.at[whole], o_ref.at[whole], sent.at[3 + d], got.at[3 + d], in_x(d), y)
-        for d in (1, 2, 3)
-    ]
-    for copy in wide:
-        copy.start()
+    spread = []
+    for t, (dx, dy) in enumerate(apart):
+        if t:
+            spread.append(
+                remote(o_ref.at[mine], o_ref.at[mine], sent.at[t], got.at[t], *place(dx, dy))
+            )
+            spread[-1].start()
     last = []
-    for d in (0, 3, 1, 2):
-        if d:
-            wide[d - 1].wait_recv()
-        piece = row(core, (x - d + 4) % 4)
-        copy = remote(o_ref.at[piece], o_ref.at[piece], sent.at[7 + d], got.at[7 + d], other_core, y)
-        copy.start()
-        last.append(copy)
+    for t, (dx, dy) in enumerate(apart):
+        if t:
+            spread[t - 1].wait_recv()
+        piece = share(core, (x - dx + 4) % 4, (y - dy + 4) % 4)
+        last.append(
+            remote(o_ref.at[piece], o_ref.at[piece], sent.at[16 + t], got.at[16 + t], other_core, y)
+        )
+        last[-1].start()
     for copy in last:
         copy.wait_recv()
-    for copy in [across] + spread + wide + last:
+    for copy in [across] + spread + last:
         copy.wait_send()
     fetch.wait()
 
@@ -364,22 +351,10 @@
     m = leaf % 16
     base = leaf - m
     core, x, z = m % 2, (m // 2) % 4, m // 8
-    me = m * 4 + y
-    barrier = pltpu.get_barrier_semaphore()
-
-    def meet(d, carry):
-        other = (me + d) % 64
-        pl.semaphore_signal(
-            barrier,
-            inc=1,
-            device_id=(base + other // 4, other % 4),
-            device_id_type=pl.DeviceIdType.MESH,
-        )
-        return carry
-
-    lax.fori_loop(1, 64, meet, 0)
     met[:, 4] = jnp.zeros((16, 8, BLK), F32)
-    pl.semaphore_wait(barrier, 63)
+    greet(
+        [(base + (m + d) % 16, y) for d in range(1, 16)] + [(leaf, (y + d) % 4) for d in (1, 2, 3)]
+    )
 
     kept = pltpu.make_async_copy(leaf_ref.at[:, m], met.at[m, 0:4], keep.at[0])
     kept.start()
@@ -391,25 +366,17 @@
         )
         members[-1].start()
     a, half = m // 2, m % 2
-    high = a // 4
-    target_y = a + high * (7 - 2 * a)
-    wide = pl.ds(pl.multiple_of(y * 256, 256), 256)
     for g in range(8):
         to = half * 8 + g
         source = entries_ref.at[pl.ds(8 * g, 8), :]
-        target = own_entries.at[high, :, wide]
-        stays = jnp.logical_and(to == m, target_y == y)
-
-        @pl.when(stays)
+
+        @pl.when(to == m)
         def _():
-            copy = pltpu.make_async_copy(source, target, got_e.at[high, y])
-            copy.start()
-
-        @pl.when(jnp.logical_not(stays))
+            pltpu.make_async_copy(source, own_entries.at[a], got_e.at[a]).start()
+
+        @pl.when(to != m)
         def _():
-            remote(
-                source, target, sent_e.at[g], got_e.at[high, y], base + to, target_y
-            ).start()
+            remote(source, own_entries.at[a], sent_e.at[g], got_e.at[a], base + to, y).start()
 
     lane = lax.broadcasted_iota(jnp.int32, (16, BLK), 1)
     group = (
@@ -442,6 +409,21 @@
         return carry
 
     lax.fori_loop(0, 36, sum_block, 0)
+    for k in range(8):
+        pltpu.make_async_copy(
+            entries_ref.at[pl.ds(0, 8), :], own_entries.at[k], got_e.at[k]
+        ).wait()
+    for k in range(8):
+        first = 9 * k if k < 4 else 9 * (7 - k) + 8 - k
+        for h in range(2):
+            b = 2 * y + h
+
+            @pl.when(b <= k)
+            def _():
+                partial[first + b] = (
+                    partial[first + b] + own_entries[k, :, h * BLK : (h + 1) * BLK]
+                )
+
     to_sum = []
     for d in (1, 2, 3):
         to = (y + d) % 4
@@ -452,22 +434,13 @@
             )
         )
         to_sum[-1].start()
-    for h in range(2):
-        for c in range(4):
-            pltpu.make_async_copy(
-                entries_ref.at[pl.ds(0, 8), :],
-                own_entries.at[h, :, pl.ds(c * 256, 256)],
-                got_e.at[h, c],
-            ).wait()
     for copy in to_sum:
         copy.wait_recv()
     rows = pl.ds(pl.multiple_of(m * 8, 8), 8)
     for t in range(9):
-        second = (t + 8 - y) // 9
-        b = t - second * (y + 1)
-        entry = own_entries[second, :, pl.ds(pl.multiple_of(b * BLK, BLK), BLK)]
-        value = partial[9 * y + t] + halves_in[0, t] + halves_in[1, t] + halves_in[2, t]
-        o_ref[9 * y + t, rows, :] = value + entry
+        o_ref[9 * y + t, rows, :] = (
+            partial[9 * y + t] + halves_in[0, t] + halves_in[1, t] + halves_in[2, t]
+        )
     spread = []
     own = o_ref.at[pl.ds(9 * y, 9), rows, :]
     for d in (1, 2, 3):
@@ -548,11 +521,11 @@
     for g in range(8):
         to = half * 8 + g
 
-        @pl.when(jnp.logical_not(jnp.logical_and(to == m, target_y == y)))
+        @pl.when(to != m)
         def _():
             remote(
-                entries_ref.at[pl.ds(8 * g, 8), :], own_entries.at[high, :, wide],
-                sent_e.at[g], got_e.at[high, y], base + to, target_y,
+                entries_ref.at[pl.ds(8 * g, 8), :], own_entries.at[a],
+                sent_e.at[g], got_e.at[a], base + to, y,
             ).wait_send()
 
 
@@ -572,11 +545,11 @@
             pltpu.VMEM((16, 5, 8, BLK), F32),
             pltpu.VMEM((36, 8, BLK), F32),
             pltpu.VMEM((3, 9, 8, BLK), F32),
-            pltpu.VMEM((2, 8, 1024), F32),
+            pltpu.VMEM((8, 8, 256), F32),
             pltpu.VMEM((16, BLK), jnp.int32),
             pltpu.SMEM((16, BLK), jnp.int32),
             dma,
-            dma((1,)), dma((16,)), dma((16,)), dma((8,)), dma((2, 4)), dma((8,)), dma((8,)),
+            dma((1,)), dma((16,)), dma((16,)), dma((8,)), dma((8,)), dma((8,)), dma((8,)),
             dma((12,)), dma((12,)), dma((16,)), dma((16,)),
         ],
         compiler_params=pltpu.CompilerParams(
@@ -593,7 +566,7 @@
         out_shape=(jax.ShapeDtypeStruct(tri.shape, F32), jax.ShapeDtypeStruct((n, n), F32)),
         in_specs=[VMEM_SPEC, pl.BlockSpec(memory_space=pltpu.HBM)],
         out_specs=(VMEM_SPEC, VMEM_SPEC),
-        scratch_shapes=[dma((11,)), dma((11,)), dma],
+        scratch_shapes=[dma((32,)), dma((32,)), dma],
         compiler_params=pltpu.CompilerParams(
             vmem_limit_bytes=(43 if collective_id == 1 else 16) * 1024 * 1024, collective_id=collective_id, has_side_effects=True
         ),
@@ -631,29 +604,39 @@
     )(maps, base, mine, other)
 
 
-def column_of_inverse(swept, sigma, sigma_left, coupling_left, block, value, value_right, column):
+def columns_of_inverse(swept, sigma, sigma_left, coupling_left, blocks, value, value_right, out):
     half = 4 * BLK
-    whole = slice(None)
-
-    @pl.when(block < 4)
-    def _():
-        put_right(value_right, whole, swept[half:, at_block(block)])
-        value[...] = -dot(sigma_left[...], value_right[...])
-        column[:half, :] = -swept[:half, at_block(block)]
-
-    @pl.when(block >= 4)
-    def _():
-        value[...] = sigma[:, at_block(block - 4)]
-        column[:half, :] = jnp.zeros((half, BLK), F32)
-
-    lower = value[...]
-    put_right(value_right, whole, lower)
-    column[:half, :] = column[:half, :] - dot(coupling_left[...], value_right[...])
-    column[half:, :] = lower
+    for t, block in enumerate(blocks):
+        here = slice(t * BLK, (t + 1) * BLK)
+
+        @pl.when(block < 4)
+        def _():
+            put_right(value_right, here, swept[half:, at_block(block)])
+            out[:half, here] = -swept[:half, at_block(block)]
+
+        @pl.when(block >= 4)
+        def _():
+            value_right[:, here] = jnp.zeros((3 * half, BLK), BF16)
+            out[:half, here] = jnp.zeros((half, BLK), F32)
+
+    width = len(blocks) * BLK
+    value[:, :width] = -dot(sigma_left[...], value_right[:, :width])
+    for t, block in enumerate(blocks):
+        here = slice(t * BLK, (t + 1) * BLK)
+
+        @pl.when(block >= 4)
+        def _():
+            value[:, here] = sigma[:, at_block(block - 4)]
+
+        lower = value[:, here]
+        put_right(value_right, here, lower)
+        out[half:, here] = lower
+    out[:half, :width] = out[:half, :width] - dot(coupling_left[...], value_right[:, :width])
 
 
 def back_kernel(
-    top_ref, mid_ref, leaf_ref, one_ref, two_ref, three_ref, o_ref, sigma, sigma_left, coupling_left, value, value_right, column, lower
+    top_ref, mid_ref, leaf_ref, one_ref, two_ref, three_ref, o_ref,
+    sigma, sigma_left, coupling_left, value, value_right, columns, lower,
 ):
     half = 4 * BLK
     whole = slice(None)
@@ -667,24 +650,20 @@
             sigma[i * BLK : (i + 1) * BLK, j * BLK : (j + 1) * BLK] = -picked
     put_left(sigma_left, whole, sigma[...])
     put_left(coupling_left, whole, two_ref[:half, half:])
-
-    def step(j, carry):
-        column_of_inverse(
-            two_ref, sigma, sigma_left, coupling_left, mid_ref[first_node, j], value, value_right, column
-        )
-        for i in range(4):
-            lower[i * BLK : (i + 1) * BLK, at_block(j)] = column[at_block(mid_ref[first_node, i]), :]
-        return carry
-
-    lax.fori_loop(0, 4, step, 0)
+    blocks = [mid_ref[first_node, j] for j in range(4)]
+    columns_of_inverse(
+        two_ref, sigma, sigma_left, coupling_left, blocks, value, value_right, columns
+    )
+    for i in range(4):
+        lower[i * BLK : (i + 1) * BLK, :] = columns[at_block(blocks[i]), :]
     put_left(sigma_left, whole, lower[...])
     put_left(coupling_left, whole, one_ref[:half, half:])
-    column_of_inverse(
-        one_ref, lower, sigma_left, coupling_left, leaf_ref[leaf, lax.axis_index("front")],
-        value, value_right, column,
+    columns_of_inverse(
+        one_ref, lower, sigma_left, coupling_left, [leaf_ref[leaf, lax.axis_index("front")]],
+        value, value_right, columns,
     )
     for i in range(4):
-        o_ref[i * BLK : (i + 1) * BLK, :] = column[at_block(leaf_ref[leaf, i]), :]
+        o_ref[i * BLK : (i + 1) * BLK, :] = columns[at_block(leaf_ref[leaf, i]), :BLK]
 
 
 def back_substituted(top, mid, leaf, one, two, three):
@@ -698,9 +677,9 @@
             pltpu.VMEM((half, half), F32),
             pltpu.VMEM((half, 3 * half), BF16),
             pltpu.VMEM((half, 3 * half), BF16),
-            pltpu.VMEM((half, BLK), F32),
-            pltpu.VMEM((3 * half, BLK), BF16),
-            pltpu.VMEM((2 * half, BLK), F32),
+            pltpu.VMEM((half, half), F32),
+            pltpu.VMEM((3 * half, half), BF16),
+            pltpu.VMEM((2 * half, half), F32),
             pltpu.VMEM((half, half), F32),
         ],
         compiler_params=PARAMS,

time: 160 us -> 157 us (0.981)
  Pallas kernels: 156 us -> 154 us
    pallas_call x1, Pallas kernels: 38.8 us -> 36.1 us  [gathered(): pl.pallas_call(gather_kernel, out_shape=jax.ShapeDtypeStruct((36, BLK, BL...]
where the time goes in v6:
time: 157 us
  Pallas kernels  154 us (98%)
  local copies, waits for them, and re-layouts  2.58 us (2%)
    pallas_call x2, Pallas kernels, next_eliminated(): pl.pallas_call(functools.partial(next_kernel, blocks, packs, members), ou...  55.5 us
    pallas_call x1, Pallas kernels, gathered(): pl.pallas_call(gather_kernel, out_shape=jax.ShapeDtypeStruct((36, BLK, BL...  36.1 us
    pallas_call x2, Pallas kernels, exchanged(): pl.pallas_call(functools.partial(exchange_kernel, distance), out_shape=(j...  35.8 us
    pallas_call x1, Pallas kernels, first_eliminated(): pl.pallas_call(functools.partial(first_kernel, blocks), out_shape=(jax.Sh...  18.5 us
    pallas_call x1, Pallas kernels, back_substituted(): pl.pallas_call(back_kernel, out_shape=jax.ShapeDtypeStruct((half, BLK), F...  7.9 us

profile of v6, /device:TPU:1, one launch (start us, length us, event | category | flops | bytes accessed | tf_op | source)
XLA Modules:
  0.0 156.6 jit_solution(15116070877837987914)
XLA Ops:
  0.0 0.8 copy.11.map_ref.leaf_ref
  0.8 0.0 copy-start.1
  0.8 0.9 copy-done.1
  1.7 0.0 copy-start.2
  1.7 0.8 copy-done.2
  2.6 36.1 %shard_map.73.lower_ref = f32[36,128,128]{2,1,0:T(8,128)S(1)} custom-call(s32[64,4]{1,0:T(8,128)S(1)} %copy.11.map_ref.leaf_ref, f32[4,16,8,128]{3,2,1,0:T(8,128)S(1)} %bitcast.1, f32[64,256]{1,0:T(8,128)S(1)} %copy-done.2), custom_call_target="tpu_custom_call" | custom-call | tf_op jit(solution)/shard_map/pallas_call | solution.py:539
  38.7 18.5 %shard_map.74 = (f32[1024,1024]{1,0:T(8,128)S(1)}, f32[1280,128]{1,0:T(8,128)S(1)}) custom-call(f32[36,128,128]{2,1,0:T(8,128)S(1)} %shard_map.73.lower_ref), custom_call_target="tpu_custom_call" | custom-call | tf_op jit(solution)/shard_map/pallas_call | solution.py:578
  57.2 0.0 copy-start.3
  57.3 18.0 %shard_map.75 = (f32[1280,128]{1,0:T(8,128)S(1)}, f32[1024,1024]{1,0:T(8,128)S(1)}) custom-call(f32[1280,128]{1,0:T(8,128)S(1)} %get-tuple-element.14.tri_ref.mine_ref, f32[2048,1024]{1,0:T(8,128)} %entries_ref.4), custom_call_target="tpu_custom_call" | custom-call | tf_op jit(solution)/shard_map/pallas_call | solution.py:564
  75.2 0.0 copy-start
  75.2 0.0 copy-done.3
  75.3 0.0 copy-start.4
  75.3 19.1 %shard_map.76 = (f32[1024,1024]{1,0:T(8,128)S(1)}, f32[1280,128]{1,0:T(8,128)S(1)}) custom-call(s32[4,4]{1,0:T(4,128)S(1)} %copy-done.3, f32[1024,1024]{1,0:T(8,128)S(1)} %get-tuple-element.15.base_ref, f32[1280,128]{1,0:T(8,128)S(1)} %get-tuple-element.14.tri_ref.mine_ref, f32[1280,128]{1,0:T(8,128)S(1)} %get-tuple-element.16.other_ref), custom_call_target="tpu_custom_call", output_to_operand_aliasing={{0}: (1, {})} | custom-call | tf_op jit(solution)/shard_map/pallas_call | solution.py:596
  94.4 0.0 copy-done
  94.4 17.8 %shard_map.77 = (f32[1280,128]{1,0:T(8,128)S(1)}, f32[1024,1024]{1,0:T(8,128)S(1)}) custom-call(f32[1280,128]{1,0:T(8,128)S(1)} %get-tuple-element.18.tri_ref.mine_ref, f32[1024,1024]{1,0:T(8,128)S(1)} %copy-done), custom_call_target="tpu_custom_call" | custom-call | tf_op jit(solution)/shard_map/pallas_call | solution.py:564
  112.3 0.0 copy-done.4
  112.3 36.4 %shard_map.78.three_ref = f32[1024,1024]{1,0:T(8,128)S(1)} custom-call(s32[2,4]{1,0:T(2,128)S(1)} %copy-done.4, f32[1024,1024]{1,0:T(8,128)S(1)} %get-tuple-element.19.base_ref, f32[1280,128]{1,0:T(8,128)S(1)} %get-tuple-element.18.tri_ref.mine_ref, f32[1280,128]{1,0:T(8,128)S(1)} %get-tuple-element.20.other_ref), custom_call_target="tpu_custom_call", output_to_operand_aliasing={{}: (1, {})} | custom-call | tf_op jit(solution)/shard_map/pallas_call | solution.py:596
  148.7 7.9 %shard_map.79 = f32[512,128]{1,0:T(8,128)} custom-call(s32[2,4]{1,0:T(2,128)S(1)} %copy-done.4, s32[4,4]{1,0:T(4,128)S(1)} %copy-done.3, s32[64,4]{1,0:T(8,128)S(1)} %copy.11.map_ref.leaf_ref, f32[1024,1024]{1,0:T(8,128)S(1)} %get-tuple-element.13.one_ref, f32[1024,1024]{1,0:T(8,128)S(1)} %get-tuple-element.17.two_ref, f32[1024,1024]{1,0:T(8,128)S(1)} %shard_map.78.three_ref), custom_call_target="tpu_custom_call" | custom-call | tf_op jit(solution)/shard_map/pallas_call | solution.py:671
Async XLA Ops:
  0.8 0.9 copy-start.1
  1.7 0.8 copy-start.2
  57.2 18.0 %copy-start.3 = (s32[4,4]{1,0:T(4,128)S(1)}, s32[4,4]{1,0:T(4,128)}, u32[]{:S(2)}) copy-start(s32[4,4]{1,0:T(4,128)} %mid_ref.1) | copy-start | bytes 196
  75.2 19.2 %copy-start = (f32[1024,1024]{1,0:T(8,128)S(1)}, f32[1024,1024]{1,0:T(8,128)}, u32[]{:S(2)}) copy-start(f32[1024,1024]{1,0:T(8,128)} %entries_ref.5) | copy-start | bytes 12582916
  75.3 37.0 %copy-start.4 = (s32[2,4]{1,0:T(2,128)S(1)}, s32[2,4]{1,0:T(2,128)}, u32[]{:S(2)}) copy-start(s32[2,4]{1,0:T(2,128)} %top_ref.1) | copy-start | bytes 100

commit v7 on v6

--- a/solution.py
+++ b/solution.py
@@ -133,7 +133,7 @@
     def turn(r, carry):
         for p in range(16 // rounds):
             carry = panel(r * (16 // rounds) + p, carry)
-            if p == 0:
+            if p == 1:
                 beside(r)
         return carry
 
@@ -264,14 +264,72 @@
             o_ref[columns, rows] = o_ref[columns, rows] + part.T
 
 
-def next_kernel(blocks, packs, members, map_ref, base_ref, mine_ref, other_ref, o_ref, *rest):
-    tri_ref, scratch = (rest[0], rest[1:]) if packs else (None, rest)
+def next_kernel(blocks, members, map_ref, base_ref, mine_ref, other_ref, o_ref, *rest):
+    tri_ref, scratch = rest[0], rest[1:]
     child = lax.axis_index("leaf") // members
     add_child(o_ref, mine_ref, map_ref, child)
     add_child(o_ref, other_ref, map_ref, child + 1 - 2 * (child % 2))
     eliminate(o_ref, blocks, *scratch)
-    if packs:
-        pack_update(o_ref, tri_ref)
+    pack_update(o_ref, tri_ref)
+
+
+def top_kernel(
+    members, map_ref, base_ref, mine_ref, other_ref, sigma_ref,
+    order, position, o, low, left, right, small_right, inverted, low_left, low_right,
+):
+    child = lax.axis_index("leaf") // members
+    other = child + 1 - 2 * (child % 2)
+    count = jnp.int32(0)
+    for b in range(8):
+        named = jnp.int32(-1)
+        for i in range(4):
+            named = jnp.where(map_ref[child, i] == b, 4 + i, named)
+        spot = jnp.where(named < 0, count, named)
+        count = count + jnp.where(named < 0, 1, 0)
+        order[spot] = b
+        position[b] = spot
+    for p in range(8):
+        for q in range(8):
+            o[p * BLK : (p + 1) * BLK, q * BLK : (q + 1) * BLK] = base_ref[
+                at_block(order[p]), at_block(order[q])
+            ]
+    half = 4 * BLK
+    for t, (i, j) in enumerate(SHARE):
+        part = mine_ref[t * BLK : (t + 1) * BLK, :]
+        rows = slice(half + i * BLK, half + (i + 1) * BLK)
+        columns = slice(half + j * BLK, half + (j + 1) * BLK)
+        o[rows, columns] = o[rows, columns] + part
+        if i != j:
+            o[columns, rows] = o[columns, rows] + part.T
+    for t, (i, j) in enumerate(SHARE):
+        part = other_ref[t * BLK : (t + 1) * BLK, :]
+        rows, columns = at_block(position[map_ref[other, i]]), at_block(position[map_ref[other, j]])
+        o[rows, columns] = o[rows, columns] + part
+        if i != j:
+            o[columns, rows] = o[columns, rows] + part.T
+    eliminate(o, 4, left, right, small_right, inverted)
+    low[...] = o[half:, half:]
+    eliminate(low, 4, low_left, low_right, small_right, inverted)
+    sigma_ref[...] = low[...]
+
+
+def top_inverse(maps, base, mine, other, members):
+    n, half = 8 * BLK, 4 * BLK
+    return pl.pallas_call(
+        functools.partial(top_kernel, members),
+        out_shape=jax.ShapeDtypeStruct((half, half), F32),
+        in_specs=[SMEM_SPEC, VMEM_SPEC, VMEM_SPEC, VMEM_SPEC],
+        out_specs=VMEM_SPEC,
+        scratch_shapes=[
+            pltpu.SMEM((8,), jnp.int32),
+            pltpu.SMEM((8,), jnp.int32),
+            pltpu.VMEM((n, n), F32),
+            pltpu.VMEM((half, half), F32),
+        ]
+        + scratch_for(n)
+        + scratch_for(half)[:2],
+        compiler_params=PARAMS,
+    )(maps, base, mine, other)
 
 
 def remote(source, target, sent, received, leaf, front):
@@ -588,16 +646,14 @@
     )(lower)
 
 
-def next_eliminated(maps, base, mine, other, blocks, packs, members):
+def next_eliminated(maps, base, mine, other, blocks, members):
     n = 8 * BLK
-    out = [jax.ShapeDtypeStruct((n, n), F32)]
-    if packs:
-        out.append(jax.ShapeDtypeStruct((10 * BLK, BLK), F32))
+    out = (jax.ShapeDtypeStruct((n, n), F32), jax.ShapeDtypeStruct((10 * BLK, BLK), F32))
     return pl.pallas_call(
-        functools.partial(next_kernel, blocks, packs, members),
-        out_shape=tuple(out),
+        functools.partial(next_kernel, blocks, members),
+        out_shape=out,
         in_specs=[SMEM_SPEC, VMEM_SPEC, VMEM_SPEC, VMEM_SPEC],
-        out_specs=tuple([VMEM_SPEC] * len(out)),
+        out_specs=(VMEM_SPEC, VMEM_SPEC),
         scratch_shapes=scratch_for(n),
         input_output_aliases={1: 0},
         compiler_params=PARAMS,
@@ -635,19 +691,14 @@
 
 
 def back_kernel(
-    top_ref, mid_ref, leaf_ref, one_ref, two_ref, three_ref, o_ref,
+    mid_ref, leaf_ref, one_ref, two_ref, top_ref, o_ref,
     sigma, sigma_left, coupling_left, value, value_right, columns, lower,
 ):
     half = 4 * BLK
     whole = slice(None)
     leaf = lax.axis_index("leaf")
-    first_node, second_node = leaf // 16, leaf // 32
-    for i in range(4):
-        for j in range(4):
-            picked = three_ref[
-                at_block(top_ref[second_node, i]), at_block(top_ref[second_node, j])
-            ]
-            sigma[i * BLK : (i + 1) * BLK, j * BLK : (j + 1) * BLK] = -picked
+    first_node = leaf // 16
+    sigma[...] = -top_ref[...]
     put_left(sigma_left, whole, sigma[...])
     put_left(coupling_left, whole, two_ref[:half, half:])
     blocks = [mid_ref[first_node, j] for j in range(4)]
@@ -666,12 +717,12 @@
         o_ref[i * BLK : (i + 1) * BLK, :] = columns[at_block(leaf_ref[leaf, i]), :BLK]
 
 
-def back_substituted(top, mid, leaf, one, two, three):
+def back_substituted(mid, leaf, one, two, top):
     half = 4 * BLK
     return pl.pallas_call(
         back_kernel,
         out_shape=jax.ShapeDtypeStruct((half, BLK), F32),
-        in_specs=[SMEM_SPEC] * 3 + [VMEM_SPEC] * 3,
+        in_specs=[SMEM_SPEC] * 2 + [VMEM_SPEC] * 3,
         out_specs=VMEM_SPEC,
         scratch_shapes=[
             pltpu.VMEM((half, half), F32),
@@ -683,7 +734,7 @@
             pltpu.VMEM((half, half), F32),
         ],
         compiler_params=PARAMS,
-    )(top, mid, leaf, one, two, three)
+    )(mid, leaf, one, two, top)
 
 
 def body(leaf_update, front_entries1, front_entries2, front_entries3, map_leaf, map_mid, map_top):
@@ -691,10 +742,10 @@
     lower = gathered(map_leaf, leaf_update, front_entries1)
     one, update = first_eliminated(lower, SEP1 // BLK)
     other, base = exchanged(update, front_entries2, members, 1)
-    two, update = next_eliminated(map_mid, base, update, other, SEP2 // BLK, True, members)
+    two, update = next_eliminated(map_mid, base, update, other, SEP2 // BLK, members)
     other, base = exchanged(update, front_entries3, 2 * members, 2)
-    (three,) = next_eliminated(map_top, base, update, other, SEP3 // BLK, False, 2 * members)
-    return back_substituted(map_top, map_mid, map_leaf, one, two, three)
+    top = top_inverse(map_top, base, update, other, 2 * members)
+    return back_substituted(map_mid, map_leaf, one, two, top)
 
 
 def solution(mesh):

time: 157 us -> 151 us (0.962)
  Pallas kernels: 154 us -> 148 us
    pallas_call x2, Pallas kernels: 55.5 us -> 50.9 us  [the longest x1 32.8 us: top_inverse(): pl.pallas_call(functools.partial(top_kernel, members), out_shape=jax.Shap...]
where the time goes in v7:
time: 151 us
  Pallas kernels  148 us (98%)
  local copies, waits for them, and re-layouts  2.58 us (2%)
    pallas_call x1, Pallas kernels, gathered(): pl.pallas_call(gather_kernel, out_shape=jax.ShapeDtypeStruct((36, BLK, BL...  36.1 us
    pallas_call x2, Pallas kernels, exchanged(): pl.pallas_call(functools.partial(exchange_kernel, distance), out_shape=(j...  35.8 us
    pallas_call x1, Pallas kernels, top_inverse(): pl.pallas_call(functools.partial(top_kernel, members), out_shape=jax.Shap...  32.8 us
    pallas_call x1, Pallas kernels, next_eliminated(): pl.pallas_call(functools.partial(next_kernel, blocks, members), out_shape...  18.1 us
    pallas_call x1, Pallas kernels, first_eliminated(): pl.pallas_call(functools.partial(first_kernel, blocks), out_shape=(jax.Sh...  17.4 us
    pallas_call x1, Pallas kernels, back_substituted(): pl.pallas_call(back_kernel, out_shape=jax.ShapeDtypeStruct((half, BLK), F...  7.67 us

profile of v7, /device:TPU:1, one launch (start us, length us, event | category | flops | bytes accessed | tf_op | source)
XLA Modules:
  0.0 150.6 jit_solution(17399701255890231418)
XLA Ops:
  0.0 0.8 copy.10.map_ref.leaf_ref
  0.8 0.0 copy-start.1
  0.8 0.9 copy-done.1
  1.7 0.0 copy-start.2
  1.7 0.8 copy-done.2
  2.6 36.1 %shard_map.73.lower_ref = f32[36,128,128]{2,1,0:T(8,128)S(1)} custom-call(s32[64,4]{1,0:T(8,128)S(1)} %copy.10.map_ref.leaf_ref, f32[4,16,8,128]{3,2,1,0:T(8,128)S(1)} %bitcast.1, f32[64,256]{1,0:T(8,128)S(1)} %copy-done.2), custom_call_target="tpu_custom_call" | custom-call | tf_op jit(solution)/shard_map/pallas_call | solution.py:597
  38.7 17.4 %shard_map.74 = (f32[1024,1024]{1,0:T(8,128)S(1)}, f32[1280,128]{1,0:T(8,128)S(1)}) custom-call(f32[36,128,128]{2,1,0:T(8,128)S(1)} %shard_map.73.lower_ref), custom_call_target="tpu_custom_call" | custom-call | tf_op jit(solution)/shard_map/pallas_call | solution.py:636
  56.2 0.0 copy-start.3
  56.2 18.0 %shard_map.75 = (f32[1280,128]{1,0:T(8,128)S(1)}, f32[1024,1024]{1,0:T(8,128)S(1)}) custom-call(f32[1280,128]{1,0:T(8,128)S(1)} %get-tuple-element.14.tri_ref.mine_ref, f32[2048,1024]{1,0:T(8,128)} %entries_ref.4), custom_call_target="tpu_custom_call" | custom-call | tf_op jit(solution)/shard_map/pallas_call | solution.py:622
  74.2 0.0 copy-start
  74.2 0.0 copy-done.3
  74.2 0.0 copy-start.4
  74.2 18.1 %shard_map.76 = (f32[1024,1024]{1,0:T(8,128)S(1)}, f32[1280,128]{1,0:T(8,128)S(1)}) custom-call(s32[4,4]{1,0:T(4,128)S(1)} %copy-done.3, f32[1024,1024]{1,0:T(8,128)S(1)} %get-tuple-element.15.base_ref, f32[1280,128]{1,0:T(8,128)S(1)} %get-tuple-element.14.tri_ref.mine_ref, f32[1280,128]{1,0:T(8,128)S(1)} %get-tuple-element.16.other_ref), custom_call_target="tpu_custom_call", output_to_operand_aliasing={{0}: (1, {})} | custom-call | tf_op jit(solution)/shard_map/pallas_call | solution.py:652
  92.3 0.0 copy-done
  92.3 17.8 %shard_map.77 = (f32[1280,128]{1,0:T(8,128)S(1)}, f32[1024,1024]{1,0:T(8,128)S(1)}) custom-call(f32[1280,128]{1,0:T(8,128)S(1)} %get-tuple-element.18.tri_ref.mine_ref, f32[1024,1024]{1,0:T(8,128)S(1)} %copy-done), custom_call_target="tpu_custom_call" | custom-call | tf_op jit(solution)/shard_map/pallas_call | solution.py:622
  110.1 0.0 copy-done.4
  110.1 32.8 %shard_map.78.top_ref = f32[512,512]{1,0:T(8,128)S(1)} custom-call(s32[2,4]{1,0:T(2,128)S(1)} %copy-done.4, f32[1024,1024]{1,0:T(8,128)S(1)} %get-tuple-element.19.base_ref, f32[1280,128]{1,0:T(8,128)S(1)} %get-tuple-element.18.tri_ref.mine_ref, f32[1280,128]{1,0:T(8,128)S(1)} %get-tuple-element.20.other_ref), custom_call_target="tpu_custom_call" | custom-call | tf_op jit(solution)/shard_map/pallas_call | solution.py:318
  143.0 7.7 %shard_map.79 = f32[512,128]{1,0:T(8,128)} custom-call(s32[4,4]{1,0:T(4,128)S(1)} %copy-done.3, s32[64,4]{1,0:T(8,128)S(1)} %copy.10.map_ref.leaf_ref, f32[1024,1024]{1,0:T(8,128)S(1)} %get-tuple-element.13.one_ref, f32[1024,1024]{1,0:T(8,128)S(1)} %get-tuple-element.17.two_ref, f32[512,512]{1,0:T(8,128)S(1)} %shard_map.78.top_ref), custom_call_target="tpu_custom_call" | custom-call | tf_op jit(solution)/shard_map/pallas_call | solution.py:722
Async XLA Ops:
  0.8 0.9 copy-start.1
  1.7 0.8 copy-start.2
  56.2 18.0 %copy-start.3 = (s32[4,4]{1,0:T(4,128)S(1)}, s32[4,4]{1,0:T(4,128)}, u32[]{:S(2)}) copy-start(s32[4,4]{1,0:T(4,128)} %mid_ref.1) | copy-start | bytes 196
  74.2 18.1 %copy-start = (f32[1024,1024]{1,0:T(8,128)S(1)}, f32[1024,1024]{1,0:T(8,128)}, u32[]{:S(2)}) copy-start(f32[1024,1024]{1,0:T(8,128)} %entries_ref.5) | copy-start | bytes 12582916
  74.2 35.9 %copy-start.4 = (s32[2,4]{1,0:T(2,128)S(1)}, s32[2,4]{1,0:T(2,128)}, u32[]{:S(2)}) copy-start(s32[2,4]{1,0:T(2,128)} %map_ref.4) | copy-start | bytes 100

commit v8 on v7

--- a/solution.py
+++ b/solution.py
@@ -174,7 +174,7 @@
     return jnp.dot(a, b, preferred_element_type=F32)
 
 
-def eliminate(o, blocks, left, right, small_right, inverted):
+def eliminate(o, blocks, left, right, small_right, inverted, begun=False, ahead=False):
     n = o.shape[0]
     whole = slice(None)
     eye = (
@@ -201,8 +201,9 @@
         these = pl.ds(pl.multiple_of(t * size, size), size)
         o[these, :] = o[these, :] - dot(left[these, :], right[...])
 
-    inverted[:BLK, :] = o[:BLK, :BLK]
-    invert(inverted, 16, nothing)
+    if not begun:
+        inverted[:BLK, :] = o[:BLK, :BLK]
+        invert(inverted, 16, nothing)
 
     def step(j, carry):
         prepare(j)
@@ -211,7 +212,9 @@
         invert(inverted, ROUNDS, functools.partial(update, n // ROUNDS))
         return carry
 
-    lax.fori_loop(0, blocks - 1, step, 0)
+    lax.fori_loop(0, blocks if ahead else blocks - 1, step, 0)
+    if ahead:
+        return
     prepare(blocks - 1)
 
     def tile(t, carry):
@@ -307,9 +310,9 @@
         o[rows, columns] = o[rows, columns] + part
         if i != j:
             o[columns, rows] = o[columns, rows] + part.T
-    eliminate(o, 4, left, right, small_right, inverted)
+    eliminate(o, 4, left, right, small_right, inverted, ahead=True)
     low[...] = o[half:, half:]
-    eliminate(low, 4, low_left, low_right, small_right, inverted)
+    eliminate(low, 4, low_left, low_right, small_right, inverted, begun=True)
     sigma_ref[...] = low[...]
 
 

time: 151 us -> 150 us (level)
  no operation moved by 1% of the time
where the time goes in v8:
time: 150 us
  Pallas kernels  147 us (98%)
  local copies, waits for them, and re-layouts  2.58 us (2%)
    pallas_call x1, Pallas kernels, gathered(): pl.pallas_call(gather_kernel, out_shape=jax.ShapeDtypeStruct((36, BLK, BL...  36.1 us
    pallas_call x2, Pallas kernels, exchanged(): pl.pallas_call(functools.partial(exchange_kernel, distance), out_shape=(j...  35.8 us
    pallas_call x1, Pallas kernels, top_inverse(): pl.pallas_call(functools.partial(top_kernel, members), out_shape=jax.Shap...  31.6 us
    pallas_call x1, Pallas kernels, next_eliminated(): pl.pallas_call(functools.partial(next_kernel, blocks, members), out_shape...  18.1 us
    pallas_call x1, Pallas kernels, first_eliminated(): pl.pallas_call(functools.partial(first_kernel, blocks), out_shape=(jax.Sh...  17.4 us
    pallas_call x1, Pallas kernels, back_substituted(): pl.pallas_call(back_kernel, out_shape=jax.ShapeDtypeStruct((half, BLK), F...  7.79 us

profile of v8, /device:TPU:1, one launch (start us, length us, event | category | flops | bytes accessed | tf_op | source)
XLA Modules:
  0.0 149.5 jit_solution(1579255790594672190)
XLA Ops:
  0.0 0.8 copy.10.map_ref.leaf_ref
  0.8 0.0 copy-start.1
  0.8 0.9 copy-done.1
  1.7 0.0 copy-start.2
  1.7 0.8 copy-done.2
  2.6 36.1 %shard_map.73.lower_ref = f32[36,128,128]{2,1,0:T(8,128)S(1)} custom-call(s32[64,4]{1,0:T(8,128)S(1)} %copy.10.map_ref.leaf_ref, f32[4,16,8,128]{3,2,1,0:T(8,128)S(1)} %bitcast.1, f32[64,256]{1,0:T(8,128)S(1)} %copy-done.2), custom_call_target="tpu_custom_call" | custom-call | tf_op jit(solution)/shard_map/pallas_call | solution.py:600
  38.7 17.4 %shard_map.74 = (f32[1024,1024]{1,0:T(8,128)S(1)}, f32[1280,128]{1,0:T(8,128)S(1)}) custom-call(f32[36,128,128]{2,1,0:T(8,128)S(1)} %shard_map.73.lower_ref), custom_call_target="tpu_custom_call" | custom-call | tf_op jit(solution)/shard_map/pallas_call | solution.py:639
  56.2 0.0 copy-start.3
  56.2 18.0 %shard_map.75 = (f32[1280,128]{1,0:T(8,128)S(1)}, f32[1024,1024]{1,0:T(8,128)S(1)}) custom-call(f32[1280,128]{1,0:T(8,128)S(1)} %get-tuple-element.14.tri_ref.mine_ref, f32[2048,1024]{1,0:T(8,128)} %entries_ref.4), custom_call_target="tpu_custom_call" | custom-call | tf_op jit(solution)/shard_map/pallas_call | solution.py:625
  74.2 0.0 copy-start
  74.2 0.0 copy-done.3
  74.2 0.0 copy-start.4
  74.2 18.1 %shard_map.76 = (f32[1024,1024]{1,0:T(8,128)S(1)}, f32[1280,128]{1,0:T(8,128)S(1)}) custom-call(s32[4,4]{1,0:T(4,128)S(1)} %copy-done.3, f32[1024,1024]{1,0:T(8,128)S(1)} %get-tuple-element.15.base_ref, f32[1280,128]{1,0:T(8,128)S(1)} %get-tuple-element.14.tri_ref.mine_ref, f32[1280,128]{1,0:T(8,128)S(1)} %get-tuple-element.16.other_ref), custom_call_target="tpu_custom_call", output_to_operand_aliasing={{0}: (1, {})} | custom-call | tf_op jit(solution)/shard_map/pallas_call | solution.py:655
  92.3 0.0 copy-done
  92.3 17.8 %shard_map.77 = (f32[1280,128]{1,0:T(8,128)S(1)}, f32[1024,1024]{1,0:T(8,128)S(1)}) custom-call(f32[1280,128]{1,0:T(8,128)S(1)} %get-tuple-element.18.tri_ref.mine_ref, f32[1024,1024]{1,0:T(8,128)S(1)} %copy-done), custom_call_target="tpu_custom_call" | custom-call | tf_op jit(solution)/shard_map/pallas_call | solution.py:625
  110.1 0.0 copy-done.4
  110.1 31.6 %shard_map.78.top_ref = f32[512,512]{1,0:T(8,128)S(1)} custom-call(s32[2,4]{1,0:T(2,128)S(1)} %copy-done.4, f32[1024,1024]{1,0:T(8,128)S(1)} %get-tuple-element.19.base_ref, f32[1280,128]{1,0:T(8,128)S(1)} %get-tuple-element.18.tri_ref.mine_ref, f32[1280,128]{1,0:T(8,128)S(1)} %get-tuple-element.20.other_ref), custom_call_target="tpu_custom_call" | custom-call | tf_op jit(solution)/shard_map/pallas_call | solution.py:321
  141.7 7.8 %shard_map.79 = f32[512,128]{1,0:T(8,128)} custom-call(s32[4,4]{1,0:T(4,128)S(1)} %copy-done.3, s32[64,4]{1,0:T(8,128)S(1)} %copy.10.map_ref.leaf_ref, f32[1024,1024]{1,0:T(8,128)S(1)} %get-tuple-element.13.one_ref, f32[1024,1024]{1,0:T(8,128)S(1)} %get-tuple-element.17.two_ref, f32[512,512]{1,0:T(8,128)S(1)} %shard_map.78.top_ref), custom_call_target="tpu_custom_call" | custom-call | tf_op jit(solution)/shard_map/pallas_call | solution.py:725
Async XLA Ops:
  0.8 0.9 copy-start.1
  1.7 0.8 copy-start.2
  56.2 18.0 %copy-start.3 = (s32[4,4]{1,0:T(4,128)S(1)}, s32[4,4]{1,0:T(4,128)}, u32[]{:S(2)}) copy-start(s32[4,4]{1,0:T(4,128)} %mid_ref.1) | copy-start | bytes 196
  74.2 18.1 %copy-start = (f32[1024,1024]{1,0:T(8,128)S(1)}, f32[1024,1024]{1,0:T(8,128)}, u32[]{:S(2)}) copy-start(f32[1024,1024]{1,0:T(8,128)} %entries_ref.5) | copy-start | bytes 12582916
  74.2 35.9 %copy-start.4 = (s32[2,4]{1,0:T(2,128)S(1)}, s32[2,4]{1,0:T(2,128)}, u32[]{:S(2)}) copy-start(s32[2,4]{1,0:T(2,128)} %map_ref.4) | copy-start | bytes 100

commit v9 on v8

--- a/solution.py
+++ b/solution.py
@@ -386,7 +386,8 @@
             spread.append(
                 remote(o_ref.at[mine], o_ref.at[mine], sent.at[t], got.at[t], *place(dx, dy))
             )
-            spread[-1].start()
+    for copy in reversed(spread):
+        copy.start()
     last = []
     for t, (dx, dy) in enumerate(apart):
         if t:

time: 150 us -> 149 us (level)
  no operation moved by 1% of the time
where the time goes in v9:
time: 149 us
  Pallas kernels  146 us (98%)
  local copies, waits for them, and re-layouts  2.58 us (2%)
    pallas_call x1, Pallas kernels, gathered(): pl.pallas_call(gather_kernel, out_shape=jax.ShapeDtypeStruct((36, BLK, BL...  36.1 us
    pallas_call x2, Pallas kernels, exchanged(): pl.pallas_call(functools.partial(exchange_kernel, distance), out_shape=(j...  34.8 us
    pallas_call x1, Pallas kernels, top_inverse(): pl.pallas_call(functools.partial(top_kernel, members), out_shape=jax.Shap...  31.7 us
    pallas_call x1, Pallas kernels, next_eliminated(): pl.pallas_call(functools.partial(next_kernel, blocks, members), out_shape...  18.1 us
    pallas_call x1, Pallas kernels, first_eliminated(): pl.pallas_call(functools.partial(first_kernel, blocks), out_shape=(jax.Sh...  17.4 us
    pallas_call x1, Pallas kernels, back_substituted(): pl.pallas_call(back_kernel, out_shape=jax.ShapeDtypeStruct((half, BLK), F...  7.8 us

profile of v9, /device:TPU:1, one launch (start us, length us, event | category | flops | bytes accessed | tf_op | source)
XLA Modules:
  0.0 148.6 jit_solution(10391562667188712994)
XLA Ops:
  0.0 0.8 copy.10.map_ref.leaf_ref
  0.8 0.0 copy-start.1
  0.8 0.9 copy-done.1
  1.7 0.0 copy-start.2
  1.7 0.8 copy-done.2
  2.6 36.1 %shard_map.73.lower_ref = f32[36,128,128]{2,1,0:T(8,128)S(1)} custom-call(s32[64,4]{1,0:T(8,128)S(1)} %copy.10.map_ref.leaf_ref, f32[4,16,8,128]{3,2,1,0:T(8,128)S(1)} %bitcast.1, f32[64,256]{1,0:T(8,128)S(1)} %copy-done.2), custom_call_target="tpu_custom_call" | custom-call | tf_op jit(solution)/shard_map/pallas_call | solution.py:601
  38.7 17.4 %shard_map.74 = (f32[1024,1024]{1,0:T(8,128)S(1)}, f32[1280,128]{1,0:T(8,128)S(1)}) custom-call(f32[36,128,128]{2,1,0:T(8,128)S(1)} %shard_map.73.lower_ref), custom_call_target="tpu_custom_call" | custom-call | tf_op jit(solution)/shard_map/pallas_call | solution.py:640
  56.2 0.0 copy-start.3
  56.2 17.1 %shard_map.75 = (f32[1280,128]{1,0:T(8,128)S(1)}, f32[1024,1024]{1,0:T(8,128)S(1)}) custom-call(f32[1280,128]{1,0:T(8,128)S(1)} %get-tuple-element.14.tri_ref.mine_ref, f32[2048,1024]{1,0:T(8,128)} %entries_ref.4), custom_call_target="tpu_custom_call" | custom-call | tf_op jit(solution)/shard_map/pallas_call | solution.py:626
  73.3 0.0 copy-start
  73.3 0.0 copy-done.3
  73.3 0.0 copy-start.4
  73.3 18.1 %shard_map.76 = (f32[1024,1024]{1,0:T(8,128)S(1)}, f32[1280,128]{1,0:T(8,128)S(1)}) custom-call(s32[4,4]{1,0:T(4,128)S(1)} %copy-done.3, f32[1024,1024]{1,0:T(8,128)S(1)} %get-tuple-element.15.base_ref, f32[1280,128]{1,0:T(8,128)S(1)} %get-tuple-element.14.tri_ref.mine_ref, f32[1280,128]{1,0:T(8,128)S(1)} %get-tuple-element.16.other_ref), custom_call_target="tpu_custom_call", output_to_operand_aliasing={{0}: (1, {})} | custom-call | tf_op jit(solution)/shard_map/pallas_call | solution.py:656
  91.4 0.0 copy-done
  91.4 17.7 %shard_map.77 = (f32[1280,128]{1,0:T(8,128)S(1)}, f32[1024,1024]{1,0:T(8,128)S(1)}) custom-call(f32[1280,128]{1,0:T(8,128)S(1)} %get-tuple-element.18.tri_ref.mine_ref, f32[1024,1024]{1,0:T(8,128)S(1)} %copy-done), custom_call_target="tpu_custom_call" | custom-call | tf_op jit(solution)/shard_map/pallas_call | solution.py:626
  109.1 0.0 copy-done.4
  109.1 31.7 %shard_map.78.top_ref = f32[512,512]{1,0:T(8,128)S(1)} custom-call(s32[2,4]{1,0:T(2,128)S(1)} %copy-done.4, f32[1024,1024]{1,0:T(8,128)S(1)} %get-tuple-element.19.base_ref, f32[1280,128]{1,0:T(8,128)S(1)} %get-tuple-element.18.tri_ref.mine_ref, f32[1280,128]{1,0:T(8,128)S(1)} %get-tuple-element.20.other_ref), custom_call_target="tpu_custom_call" | custom-call | tf_op jit(solution)/shard_map/pallas_call | solution.py:321
  140.8 7.8 %shard_map.79 = f32[512,128]{1,0:T(8,128)} custom-call(s32[4,4]{1,0:T(4,128)S(1)} %copy-done.3, s32[64,4]{1,0:T(8,128)S(1)} %copy.10.map_ref.leaf_ref, f32[1024,1024]{1,0:T(8,128)S(1)} %get-tuple-element.13.one_ref, f32[1024,1024]{1,0:T(8,128)S(1)} %get-tuple-element.17.two_ref, f32[512,512]{1,0:T(8,128)S(1)} %shard_map.78.top_ref), custom_call_target="tpu_custom_call" | custom-call | tf_op jit(solution)/shard_map/pallas_call | solution.py:726
Async XLA Ops:
  0.8 0.9 copy-start.1
  1.7 0.8 copy-start.2
  56.2 17.1 %copy-start.3 = (s32[4,4]{1,0:T(4,128)S(1)}, s32[4,4]{1,0:T(4,128)}, u32[]{:S(2)}) copy-start(s32[4,4]{1,0:T(4,128)} %mid_ref.1) | copy-start | bytes 196
  73.3 18.1 %copy-start = (f32[1024,1024]{1,0:T(8,128)S(1)}, f32[1024,1024]{1,0:T(8,128)}, u32[]{:S(2)}) copy-start(f32[1024,1024]{1,0:T(8,128)} %entries_ref.5) | copy-start | bytes 12582916
  73.3 35.8 %copy-start.4 = (s32[2,4]{1,0:T(2,128)S(1)}, s32[2,4]{1,0:T(2,128)}, u32[]{:S(2)}) copy-start(s32[2,4]{1,0:T(2,128)} %map_ref.4) | copy-start | bytes 100
